TPU v7x, 32 devices: a whole 2x2x4 slice. The times are simulated.
32 devices in a mesh: freq: 4 (over x, core), rcv: 8 (over z, y).
Axes of the slice: x: 2, y: 2, z: 4, core: 2. Of those that a mesh axis runs over, the one named last changes fastest.
Arguments:
- reflection: bfloat16 [8, 2, 2560, 2560], P('freq', None, 'rcv'), may hold values from -5 to 5, as said below
- starts: int32 [2560, 192], P('rcv'), may hold values from 8 to 56
- focusing: float32 [8, 2560, 2, 192], P('freq', 'rcv'), may hold values from -6 to 6
- residual: float32 [8, 2560, 2, 192], P('freq', 'rcv'), may hold values from -6 to 6
- direction: float32 [8, 2560, 2, 192], P('freq', 'rcv'), may hold values from -6 to 6
- gradient: float32 [8, 2560, 2, 192], P('freq', 'rcv'), may hold values from -30 to 30
Outputs:
- new_focusing: float32 [8, 2560, 2, 192], P('freq', 'rcv')
- new_residual: float32 [8, 2560, 2, 192], P('freq', 'rcv')
- new_direction: float32 [8, 2560, 2, 192], P('freq', 'rcv')
- green_field: float32 [8, 2560, 2, 192], P('freq', 'rcv')
- focal_correlation: float32 [8, 2, 192], P('freq')
Inputs may be any that keep to these rules, and one draw needn't show every extreme that they name: Each frequency's matrix is symmetric in source and receiver: reflection[f, c, s, r] = reflection[f, c, r, s].
All inputs are finite; a program needn't handle non-finite values.
Results may differ from a plain program's by a relative error of at most 0.0003.
The roundings to bfloat16 on the way count: a program that leaves them out, or rounds other values in their place, can miss the bound.
Values may be sent and summed in bfloat16 or wider, within the bound.
No kernel may reach another device: no remote copies, remote signals or barrier semaphores. Data moves between devices by JAX's collectives and lax.ppermute only.
A program may use at most 64 MiB of HBM per device.

v0:
```python
import math

import jax
import jax.numpy as jnp
from jax import lax
from jax.experimental import pallas as pl
from jax.experimental.pallas import tpu as pltpu
from jax.sharding import PartitionSpec as P


TS = 64
band_start = 5
tiny = 1e-06
highest = lax.Precision.HIGHEST
LANES = 128
HALF = 64
SINE = [(-1.0) ** i / math.factorial(2 * i + 1) for i in range(7)]
COSINE = [(-1.0) ** i / math.factorial(2 * i) for i in range(8)]


VMEM = pl.BlockSpec(memory_space=pltpu.VMEM)
SMEM = pl.BlockSpec(memory_space=pltpu.SMEM)
ANY = pl.BlockSpec(memory_space=pl.ANY)


def tables(count):
    times = jnp.arange(TS, dtype=jnp.float32)[:, None]
    bins = (jnp.arange(count, dtype=jnp.int32) + band_start).astype(jnp.float32)[None, :]
    phase = 2.0 * jnp.pi * times * bins / TS
    return (jnp.cos(phase), jnp.sin(phase))


def contract_time(table, values):
    return jnp.einsum("tf,frk->trk", table, values, precision=highest)


def contract_back(table, values):
    return jnp.einsum("tf,trk->frk", table, values, precision=highest)


def time_gate(field, cos_table, sin_table, limits, complement):
    real_part = field[:, :, 0]
    imag_part = field[:, :, 1]
    time_real = contract_time(cos_table, real_part) - contract_time(sin_table, imag_part)
    time_imag = contract_time(sin_table, real_part) + contract_time(cos_table, imag_part)
    clock = jnp.arange(TS, dtype=jnp.int32)[:, None, None]
    window = (clock < limits[None]).astype(jnp.float32)
    if complement:
        window = 1.0 - window
    kept_real = window * time_real
    kept_imag = window * time_imag
    out_real = (contract_back(cos_table, kept_real) + contract_back(sin_table, kept_imag)) / TS
    out_imag = (contract_back(cos_table, kept_imag) - contract_back(sin_table, kept_real)) / TS
    return jnp.stack([out_real, out_imag], axis=2)


def combine(total, conjugate):
    if conjugate:
        out_real = total[:, 0, :, 0] + total[:, 1, :, 1]
        out_imag = total[:, 0, :, 1] - total[:, 1, :, 0]
    else:
        out_real = total[:, 0, :, 0] - total[:, 1, :, 1]
        out_imag = total[:, 0, :, 1] + total[:, 1, :, 0]
    return jnp.stack([out_real, out_imag], axis=2)


def per_device_general(reflection, starts, focusing, residual, direction, gradient):
    local_rows = reflection.shape[2]
    positions = reflection.shape[3]
    groups = lax.axis_size("freq")
    position = lax.axis_index("freq")
    cos_table, sin_table = tables(reflection.shape[0] * groups)

    def gate(field, complement):
        spread = lax.all_to_all(field, "freq", split_axis=1, concat_axis=0, tiled=True)
        share = local_rows // groups
        limits = lax.dynamic_slice_in_dim(starts, position * share, share, 0)
        gated_part = time_gate(spread, cos_table, sin_table, limits, complement)
        return lax.all_to_all(gated_part, "freq", split_axis=0, concat_axis=1, tiled=True)

    def accumulate(piece):
        return jnp.einsum("fpnm,fmqk->fpnqk", reflection, piece, preferred_element_type=jnp.float32)

    direction_low = direction.astype(jnp.bfloat16)
    focusing_low = focusing.astype(jnp.bfloat16)
    aimed_total = accumulate(lax.all_gather(direction_low, "rcv", axis=1, tiled=True))
    direction_image = combine(aimed_total, False)
    gamma = lax.psum(jnp.sum(gradient * gradient), ("freq", "rcv"))
    image = gate(direction_image, False)
    curvature = lax.psum(jnp.sum(image * image), ("freq", "rcv"))
    alpha = gamma / (curvature + tiny)
    new_focusing = focusing + alpha * direction
    new_residual = residual - alpha * image
    gated = gate(new_residual, False).astype(jnp.bfloat16)
    total = accumulate(lax.all_gather(gated, "rcv", axis=1, tiled=True))
    new_gradient = combine(total, True)
    new_gamma = lax.psum(jnp.sum(new_gradient * new_gradient), ("freq", "rcv"))
    new_direction = new_gradient + new_gamma / (gamma + tiny) * direction
    focus_total = accumulate(lax.all_gather(focusing_low, "rcv", axis=1, tiled=True))
    focusing_image = combine(focus_total, False)
    green_field = gate(focusing_image + alpha * direction_image, True)
    corr_real = jnp.sum(
        green_field[:, :, 0] * new_focusing[:, :, 0] + green_field[:, :, 1] * new_focusing[:, :, 1],
        axis=1,
    )
    corr_imag = jnp.sum(
        green_field[:, :, 1] * new_focusing[:, :, 0] - green_field[:, :, 0] * new_focusing[:, :, 1],
        axis=1,
    )
    partial_corr = jnp.stack([corr_real, corr_imag], axis=1)
    focal_correlation = lax.psum(partial_corr, "rcv") / math.sqrt(positions)
    return (new_focusing, new_residual, new_direction, green_field, focal_correlation)


def split_row(x, odd):
    main = x.shape[-1] - HALF
    return (x[:, HALF:], x[:, :HALF]) if odd else (x[:, :main], x[:, main:])


def pack(real, imag, odd):
    (r_main, r_tail), (i_main, i_tail) = split_row(real, odd), split_row(imag, odd)
    return jnp.concatenate([r_main, i_main, jnp.concatenate([r_tail, i_tail], axis=1)], axis=1)


def unpack(row, plane, odd):
    main = row.shape[-1] // 2 - HALF
    tail = 2 * main + plane * HALF
    parts = [row[:, plane * main : (plane + 1) * main], row[:, tail : tail + HALF]]
    return jnp.concatenate(parts[::-1] if odd else parts, axis=1)


def by_parity(pos_ref, body):
    for odd in range(2):
        pl.when(pos_ref[1] == odd)(lambda odd=odd: body(odd))


def cost(flops, size):
    return pl.CostEstimate(flops=int(flops), bytes_accessed=int(size), transcendentals=0)


def prep_low_kernel(pos_ref, x_ref, o_ref):
    def body(odd):
        for f in range(x_ref.shape[0]):
            o_ref[f] = pack(x_ref[f, 0], x_ref[f, 1], odd).astype(jnp.bfloat16)

    by_parity(pos_ref, body)


def prep_low(pos, x):
    loc, _, k, n = x.shape
    return pl.pallas_call(
        prep_low_kernel,
        out_shape=jax.ShapeDtypeStruct((loc, k, 2 * n), jnp.bfloat16),
        in_specs=[SMEM, VMEM],
        out_specs=VMEM,
        cost_estimate=cost(x.size, 6 * x.size),
        name="prep_low",
    )(pos, x)


def share_of(me, p, groups):
    if groups & (groups - 1) == 0:
        return me ^ p
    return lax.rem(p - me + groups, groups)


def prep_shares_kernel(groups, pos_ref, x_ref, g_ref, *o_refs):
    me = pos_ref[0]
    ks = x_ref.shape[2] // groups

    def body(odd):
        for p in range(groups):
            at = pl.multiple_of(share_of(me, p, groups) * ks, ks)
            for f in range(x_ref.shape[0]):
                real, imag = x_ref[f, 0, pl.ds(at, ks), :], x_ref[f, 1, pl.ds(at, ks), :]
                o_refs[p][f] = pack(real, imag, odd)

    by_parity(pos_ref, body)
    total = jnp.zeros((8, g_ref.shape[3]), jnp.float32)
    for f in range(g_ref.shape[0]):
        for c in range(2):
            for r in range(0, g_ref.shape[2], 8):
                v = g_ref[f, c, r : r + 8, :]
                total = total + v * v
    o_refs[groups][...] = lane_fold(jnp.sum(total, axis=0, keepdims=True))


def lane_fold(row, width=LANES):
    out = jnp.sum(row, axis=1, keepdims=True)
    lane = lax.broadcasted_iota(jnp.int32, (1, width), 1)
    return jnp.where(lane == 0, out, 0.0)


def prep_shares(pos, x, g, groups):
    loc, _, k, n = x.shape
    outs = [jax.ShapeDtypeStruct((loc, k // groups, 2 * n), jnp.float32)] * groups
    return pl.pallas_call(
        lambda *refs: prep_shares_kernel(groups, *refs),
        out_shape=outs + [jax.ShapeDtypeStruct((1, LANES), jnp.float32)],
        in_specs=[SMEM, VMEM, VMEM],
        out_specs=[VMEM] * (groups + 1),
        cost_estimate=cost(3 * x.size, 12 * x.size),
        name="prep_shares",
    )(pos, x, g)


def product_kernel(groups, count, conjugate, pos_ref, r_ref, *refs):
    blocks, refs = refs[: 2 * count], refs[2 * count :]
    v_scr, acc = refs[-2:]
    f = pl.program_id(0)
    _, kc, wide = blocks[0].shape
    rows = r_ref.shape[2]
    main = wide // 2 - HALF

    def load(odd):
        for b in range(count):
            even = blocks[2 * b + odd]
            other = blocks[2 * b + 1 - odd]
            at = pos_ref[2 + b] * wide
            for c in range(2):
                here = slice(c * kc, (c + 1) * kc)
                half = slice(2 * main + c * HALF, 2 * main + (c + 1) * HALF)
                lanes = lambda shift, size: pl.ds(pl.multiple_of(at + shift, LANES), size)
                v_scr[here, lanes(0, main)] = even[0, :, c * main : (c + 1) * main]
                middle = [even[0, :, half], other[0, :, half]]
                v_scr[here, lanes(main, LANES)] = jnp.concatenate(middle, axis=1)
                v_scr[here, lanes(main + LANES, main)] = other[0, :, c * main : (c + 1) * main]

    by_parity(pos_ref, load)
    both = r_ref[0].reshape(2 * rows, r_ref.shape[3])
    dims = (((1,), (1,)), ((), ()))
    acc[...] = lax.dot_general(v_scr[...], both, dims, preferred_element_type=jnp.float32)
    if not conjugate:
        me = pos_ref[0]
        ks = kc // groups

        def finish(odd):
            for p in range(groups):
                at = pl.multiple_of(share_of(me, p, groups) * ks, ks)
                real = acc[pl.ds(at, ks), :rows] - acc[pl.ds(at + kc, ks), rows:]
                imag = acc[pl.ds(at + kc, ks), :rows] + acc[pl.ds(at, ks), rows:]
                refs[p][0] = pack(real, imag, odd)

        by_parity(pos_ref, finish)
    else:
        new_ref, row_ref, sum_scr = refs[:3]
        real = acc[:kc, :rows] + acc[kc:, rows:]
        imag = acc[kc:, :rows] - acc[:kc, rows:]
        new_ref[0, 0] = real
        new_ref[0, 1] = imag
        part = jnp.sum(real * real + imag * imag, axis=0, keepdims=True)

        @pl.when(f == 0)
        def _():
            sum_scr[...] = part

        @pl.when(f > 0)
        def _():
            sum_scr[...] += part

        @pl.when(f == pl.num_programs(0) - 1)
        def _():
            row_ref[...] = lane_fold(sum_scr[...])


def product(pos, reflection, blocks, groups, back=False):
    loc, _, rows, cols = reflection.shape
    kc, wide = blocks[0].shape[1:]
    count = len(blocks) // 2
    whole = lambda *tail: pl.BlockSpec((1,) + tail, lambda f, pos: (f,) + (0,) * len(tail))
    fixed = lambda *shape: pl.BlockSpec(shape, lambda f, pos: (0,) * len(shape))
    in_specs = [whole(2, rows, cols)] + [whole(kc, wide)] * (2 * count)
    operands = [pos, reflection] + list(blocks)
    scratch = []
    if not back:
        ks = kc // groups
        out_shape = [jax.ShapeDtypeStruct((loc, ks, wide), jnp.float32)] * groups
        out_specs = [whole(ks, wide)] * groups
    else:
        out_shape = [
            jax.ShapeDtypeStruct((loc, 2, kc, rows), jnp.float32),
            jax.ShapeDtypeStruct((1, LANES), jnp.float32),
        ]
        out_specs = [whole(2, kc, rows), fixed(1, LANES)]
        scratch = [pltpu.VMEM((1, rows), jnp.float32)]
    return pl.pallas_call(
        lambda *refs: product_kernel(groups, count, back, *refs),
        grid_spec=pltpu.PrefetchScalarGridSpec(
            num_scalar_prefetch=1,
            grid=(loc,),
            in_specs=in_specs,
            out_specs=out_specs,
            scratch_shapes=scratch
            + [
                pltpu.VMEM((2 * kc, cols), jnp.bfloat16),
                pltpu.VMEM((2 * kc, 2 * rows), jnp.float32),
            ],
        ),
        out_shape=out_shape,
        cost_estimate=cost(8 * loc * rows * kc * cols, 2 * reflection.size + 4 * loc * kc * cols),
        compiler_params=pltpu.CompilerParams(dimension_semantics=("arbitrary",)),
        name="product_back" if back else "product",
    )(*operands)


def turn_of(limit):
    x = (limit - TS / 2) * (math.pi / TS)
    y = x * x
    sine = jnp.full_like(y, SINE[-1])
    for v in SINE[-2::-1]:
        sine = sine * y + v
    sine = sine * x
    cosine = jnp.full_like(y, COSINE[-1])
    for v in COSINE[-2::-1]:
        cosine = cosine * y + v
    return 2.0 * sine * sine - 1.0, -2.0 * sine * cosine


def gate_weights(limit, count):
    c1, s1 = turn_of(limit)
    real = [limit * (1.0 / TS)]
    imag = [None]
    c, s = c1, s1
    for d in range(1, count):
        half_cot = 0.5 / math.tan(math.pi * d / TS)
        rest = 1.0 - c
        real.append((0.5 * rest + half_cot * s) * (1.0 / TS))
        imag.append((half_cot * rest - 0.5 * s) * (1.0 / TS))
        c, s = c * c1 - s * s1, s * c1 + c * s1
    return real, imag


def gate_pair(real, imag, ur, ui):
    count = len(ur)
    out_r, out_i = [], []
    for j in range(count):
        r = real[0] * ur[j]
        i = real[0] * ui[j]
        for m in range(count):
            d = abs(m - j)
            if m > j:
                r = r + real[d] * ur[m] - imag[d] * ui[m]
                i = i + real[d] * ui[m] + imag[d] * ur[m]
            elif m < j:
                r = r + real[d] * ur[m] + imag[d] * ui[m]
                i = i + real[d] * ui[m] - imag[d] * ur[m]
        out_r.append(r)
        out_i.append(i)
    return out_r, out_i


def gate_tail(real, signed, u):
    count = len(u)
    w = [pltpu.roll(v, HALF, 1) for v in u]
    outs = []
    for j in range(count):
        r = real[0] * u[j]
        for m in range(count):
            d = abs(m - j)
            if m > j:
                r = r + real[d] * u[m] + signed[d] * w[m]
            elif m < j:
                r = r + real[d] * u[m] - signed[d] * w[m]
        outs.append(r)
    return outs


def gate_kernel(groups, squares, mixed, pos_ref, s_ref, *refs):
    if squares:
        row_ref, refs = refs[0], refs[1:]
    if mixed:
        t_ref, bases, refs = refs[0], refs[1 : 1 + groups], refs[1 + groups :]
    ins = refs[:groups]
    outs = refs[groups : 2 * groups]
    rest = refs[2 * groups :]
    if squares:
        sum_ref, acc = rest[0], rest[1]
        rest = rest[2:]
        acc[...] = jnp.zeros_like(acc)
    u_scr, o_scr, lim_scr = rest
    me = pos_ref[0]
    loc, ks, wide = ins[0].shape
    count = groups * loc
    main = wide // 2 - HALF
    at = pl.multiple_of(me * ks, ks)
    lim = jnp.clip(s_ref[pl.ds(at, ks), :], 0, TS).astype(jnp.float32)

    def place(odd):
        whole, ends = split_row(lim, odd)
        lim_scr[:, :main] = whole
        lim_scr[:, main:] = jnp.concatenate([ends, ends], axis=1)

    by_parity(pos_ref, place)
    for p in range(groups):
        base = share_of(me, p, groups) * loc
        for f in range(loc):
            u_scr[base + f] = ins[p][f]

    def tile(i, carry):
        rows = pl.ds(pl.multiple_of(i * 8, 8), 8)
        for t in range(main // LANES + 1):
            real, imag = gate_weights(lim_scr[rows, t * LANES : (t + 1) * LANES], count)
            if t * LANES < main:
                re_at = slice(t * LANES, (t + 1) * LANES)
                im_at = slice(main + t * LANES, main + (t + 1) * LANES)
                ur = [u_scr[j, rows, re_at] for j in range(count)]
                ui = [u_scr[j, rows, im_at] for j in range(count)]
                out_r, out_i = gate_pair(real, imag, ur, ui)
                for j in range(count):
                    o_scr[j, rows, re_at] = out_r[j]
                    o_scr[j, rows, im_at] = out_i[j]
                    if squares:
                        acc[...] += out_r[j] * out_r[j] + out_i[j] * out_i[j]
            else:
                ends = slice(2 * main, 2 * main + LANES)
                lane = lax.broadcasted_iota(jnp.int32, (8, LANES), 1)
                sign = jnp.where(lane < HALF, -1.0, 1.0)
                signed = [None] + [v * sign for v in imag[1:]]
                out = gate_tail(real, signed, [u_scr[j, rows, ends] for j in range(count)])
                for j in range(count):
                    o_scr[j, rows, ends] = out[j]
                    if squares:
                        acc[...] += out[j] * out[j]
        return carry

    lax.fori_loop(0, ks // 8, tile, 0)
    for p in range(groups):
        base = share_of(me, p, groups) * loc
        for f in range(loc):
            if mixed:
                mix = bases[p][f] - alpha_of(t_ref)[0] * o_scr[base + f]
                outs[p][f] = mix.astype(jnp.bfloat16)
            else:
                outs[p][f] = o_scr[base + f]
    if squares:
        mine = lane_fold(jnp.sum(acc[...], axis=0, keepdims=True))
        both = jnp.concatenate([mine, row_ref[...]], axis=0)
        sum_ref[...] = jnp.broadcast_to(both[None], sum_ref.shape)


def gate(pos, limits, shares, groups, row=None, devices=0, sums=None, bases=()):
    squares = row is not None
    loc, ks, wide = shares[0].shape
    kind = jnp.bfloat16 if bases else jnp.float32
    out_shape = [jax.ShapeDtypeStruct((loc, ks, wide), kind)] * groups
    scratch = []
    more = []
    if squares:
        out_shape = out_shape + [jax.ShapeDtypeStruct((devices, 2, LANES), jnp.float32)]
        scratch = [pltpu.VMEM((8, LANES), jnp.float32)]
        more = [row]
    if bases:
        more = [sums, *bases]
    scratch = scratch + [
        pltpu.VMEM((groups * loc, ks, wide), jnp.float32),
        pltpu.VMEM((groups * loc, ks, wide), jnp.float32),
        pltpu.VMEM((ks, wide // 2 + HALF), jnp.float32),
    ]
    size = groups * loc * ks * wide
    return pl.pallas_call(
        lambda *refs: gate_kernel(groups, squares, bool(bases), *refs),
        out_shape=out_shape,
        in_specs=[SMEM, VMEM] + [VMEM] * (groups + len(more)),
        out_specs=[VMEM] * len(out_shape),
        scratch_shapes=scratch,
        cost_estimate=cost(40 * size, 8 * size),
        name="gate_sum" if squares else "gate_mix" if bases else "gate",
    )(pos, limits, *more, *shares)


def alpha_of(t_ref):
    gamma = jnp.sum(t_ref[:, 1, :])
    curvature = jnp.sum(t_ref[:, 0, :])
    return gamma / (curvature + tiny), gamma


def join_kernel(groups, pos_ref, *refs):
    me = pos_ref[0]
    ks = refs[0].shape[1]
    for p in range(groups):
        at = pl.multiple_of(share_of(me, p, groups) * ks, ks)
        for f in range(refs[p].shape[0]):
            refs[groups][f, pl.ds(at, ks), :] = refs[p][f]


def join(pos, shares, groups):
    loc, ks, wide = shares[0].shape
    return pl.pallas_call(
        lambda *refs: join_kernel(groups, *refs),
        out_shape=jax.ShapeDtypeStruct((loc, groups * ks, wide), shares[0].dtype),
        in_specs=[SMEM] + [VMEM] * groups,
        out_specs=VMEM,
        cost_estimate=cost(0, 4 * groups * shares[0].size),
        name="join",
    )(pos, *shares)


def finish_kernel(groups, pos_ref, t_ref, res_ref, foc_ref, dir_ref, *refs):
    row_ref, refs = refs[0], refs[1:]
    image, kept, di, fi = [refs[i * groups : (i + 1) * groups] for i in range(4)]
    nres_ref, nfoc_ref, green_ref, sent_ref, corr_scr = refs[4 * groups :]
    alpha, _ = alpha_of(t_ref)
    me = pos_ref[0]
    loc, ks, _ = di[0].shape
    nfoc_ref[...] = foc_ref[...] + alpha * dir_ref[...]

    def body(odd):
        for p in range(groups):
            rows = pl.ds(pl.multiple_of(share_of(me, p, groups) * ks, ks), ks)
            for f in range(loc):
                seen = image[p][f]
                row = (fi[p][f] - kept[p][f]) + alpha * (di[p][f] - seen)
                for c in range(2):
                    green_ref[f, c, rows, :] = unpack(row, c, odd)
                    nres_ref[f, c, rows, :] = res_ref[f, c, rows, :] - alpha * unpack(seen, c, odd)

    by_parity(pos_ref, body)
    ones = jnp.ones((8, dir_ref.shape[3]), jnp.float32)
    dims = (((1,), (1,)), ((), ()))
    for f in range(loc):
        gr, gi, fr, fm = green_ref[f, 0], green_ref[f, 1], nfoc_ref[f, 0], nfoc_ref[f, 1]
        for c, value in enumerate((gr * fr + gi * fm, gi * fr - gr * fm)):
            line = lax.dot_general(ones, value, dims, precision=highest, preferred_element_type=jnp.float32)
            corr_scr[2 * f + c : 2 * f + c + 1, :] = line[:1]
    total = jnp.broadcast_to(row_ref[:, :HALF], (2 * loc, HALF))
    ends = jnp.concatenate([corr_scr[:, LANES:], total], axis=1)
    table = jnp.concatenate([corr_scr[:, :LANES], ends], axis=0)
    sent_ref[...] = jnp.broadcast_to(table[None], sent_ref.shape)


def finish(pos, sums, residual, focusing, direction, row, image, kept, di, fi, groups):
    loc, _, k, _ = residual.shape
    size = residual.size
    return pl.pallas_call(
        lambda *refs: finish_kernel(groups, *refs),
        out_shape=[jax.ShapeDtypeStruct(residual.shape, jnp.float32)] * 3
        + [jax.ShapeDtypeStruct((sums.shape[0], 4 * loc, LANES), jnp.float32)],
        in_specs=[SMEM] + [VMEM] * (5 + 4 * groups),
        out_specs=[VMEM] * 4,
        scratch_shapes=[pltpu.VMEM((2 * loc, k), jnp.float32)],
        cost_estimate=cost(14 * size, 40 * size),
        name="finish",
    )(pos, sums, residual, focusing, direction, row, *image, *kept, *di, *fi)


def turn(pos, sums, new_sums, new_gradient, direction, ranks):
    loc, _, points, n = direction.shape
    size = direction.size
    lines = 2 * loc
    scale = 1.0 / math.sqrt(n * ranks)

    def body(pos_ref, t_ref, g_ref, new_ref, dir_ref, out_ref, corr_ref):
        _, gamma = alpha_of(t_ref)
        beta = jnp.sum(g_ref[:, lines, HALF:]) / (gamma + tiny)
        out_ref[...] = new_ref[...] + beta * dir_ref[...]
        total = jnp.zeros((2 * lines, LANES), jnp.float32)
        for r in range(ranks):
            total = total + g_ref[pos_ref[0] * ranks + r]
        total = jnp.concatenate([total[:lines], total[lines:, :HALF]], axis=1) * scale
        for f in range(loc):
            corr_ref[f] = total[2 * f : 2 * f + 2]

    return pl.pallas_call(
        body,
        in_specs=[SMEM] + [VMEM] * 4,
        out_specs=[VMEM] * 2,
        out_shape=[
            jax.ShapeDtypeStruct(direction.shape, jnp.float32),
            jax.ShapeDtypeStruct((loc, 2, points), jnp.float32),
        ],
        cost_estimate=cost(2 * size, 12 * size),
        name="turn",
    )(pos, sums, new_sums, new_gradient, direction)


def exchange(shares, groups):
    out = [shares[0]]
    for p in range(1, groups):
        pairs = [(m, share_of(m, p, groups) if groups & (groups - 1) == 0 else (p - m) % groups) for m in range(groups)]
        out.append(lax.ppermute(shares[p], "freq", pairs))
    return out


def side(deep, pick):
    pairs = []
    for z in range(deep):
        for y in range(2):
            to = pick(z, y)
            if to is not None:
                pairs.append((z * 2 + y, to[0] * 2 + to[1]))
    return pairs


def spread(own, mid):
    swap = side(4, lambda z, y: (z, 1 - y))
    near = side(4, lambda z, y: (z ^ 1, y))
    centre = side(4, lambda z, y: (3 - z, y) if z in (1, 2) else None)
    outward = side(4, lambda z, y: (0 if z == 1 else 3, y) if z in (1, 2) else None)

    def move(v, pairs):
        return lax.ppermute(v, "rcv", pairs)

    n1 = move(own, near)
    c1 = move(own, centre)
    y0 = move(own, swap)
    c2 = move(n1, centre)
    y1 = move(n1, swap)
    o1 = move(c1, outward)
    before = yield
    if before is not None:
        c2, o1, before = lax.optimization_barrier((c2, o1, before))
    yield before
    m1 = jnp.where(mid, c1, o1)
    y2 = move(m1, swap)
    o2 = move(c2, outward)
    m2 = jnp.where(mid, c2, o2)
    y3 = move(m2, swap)
    yield [own, y0, n1, y1, m1, y2, m2, y3]


def spread_all(own, mid):
    return list(spread(own, mid))[-1]


def total_over_all(sent):
    return lax.all_to_all(sent, ("freq", "rcv"), split_axis=0, concat_axis=0, tiled=True)


def per_device(reflection, starts, focusing, residual, direction, gradient):
    groups = lax.axis_size("freq")
    ranks = lax.axis_size("rcv")
    lay = lambda v: jnp.transpose(v, (0, 2, 3, 1))
    focusing, residual, direction, gradient = map(lay, (focusing, residual, direction, gradient))
    limits = jnp.transpose(starts, (1, 0))
    me = lax.axis_index("freq")
    rank = lax.axis_index("rcv")
    z, y = rank // 2, rank % 2
    mid = (z == 1) | (z == 2)
    far1 = jnp.where(z < 2, 2, 1)
    far2 = jnp.where(z < 2, 3, 0)
    pos = jnp.stack([me, y, z, z ^ 1, far1, far2]).astype(jnp.int32)

    blocks = spread_all(prep_low(pos, direction), mid)
    *res_shares, gamma_row = prep_shares(pos, residual, gradient, groups)
    res_there = exchange(res_shares, groups)
    kept_res = gate(pos, limits, res_there, groups)
    foc_own = prep_low(pos, focusing)
    aside = spread(foc_own, mid)
    next(aside)
    di = product(pos, reflection, blocks, groups)
    *image_there, sent = gate(pos, limits, exchange(di, groups), groups, gamma_row, groups * ranks)
    sums = total_over_all(sent)
    sums = aside.send(sums)
    foc = next(aside)
    gated_there = gate(pos, limits, image_there, groups, sums=sums, bases=kept_res)
    gated = join(pos, exchange(gated_there, groups), groups)
    blocks = spread_all(gated, mid)

    fi = product(pos, reflection, foc, groups)
    kept = gate(pos, limits, exchange(fi, groups), groups)
    kept = exchange(kept, groups)
    image = exchange(image_there, groups)
    new_gradient, row = product(pos, reflection, blocks, groups, True)
    new_residual, new_focusing, green_field, new_sent = finish(
        pos, sums, residual, focusing, direction, row, image, kept, di, fi, groups
    )
    new_sums = total_over_all(new_sent)
    new_direction, focal_correlation = turn(pos, sums, new_sums, new_gradient, direction, ranks)
    back = lambda v: jnp.transpose(v, (0, 3, 1, 2))
    return (back(new_focusing), back(new_residual), back(new_direction), back(green_field), focal_correlation)


def chosen(mesh):
    def run(reflection, starts, *fields):
        rows, points = starts.shape
        suits = (
            mesh.shape["rcv"] == 8
            and rows % LANES == HALF
            and rows > LANES
            and points % (16 * mesh.shape["freq"]) == 0
            and points == LANES + HALF
        )
        plan = per_device if suits else per_device_general
        return plan(reflection, starts, *fields)

    return run


def solution(mesh):
    return jax.shard_map(
        chosen(mesh),
        mesh=mesh,
        in_specs=(
            P("freq", None, "rcv", None),
            P("rcv", None),
            P("freq", "rcv", None, None),
            P("freq", "rcv", None, None),
            P("freq", "rcv", None, None),
            P("freq", "rcv", None, None),
        ),
        out_specs=(
            P("freq", "rcv", None, None),
            P("freq", "rcv", None, None),
            P("freq", "rcv", None, None),
            P("freq", "rcv", None, None),
            P("freq", None, None),
        ),
        check_vma=False,
    )
```

profile of v0, /device:TPU:0, one launch (start us, length us, event | category | flops | bytes accessed | tf_op | source)
XLA Modules:
  0.0 249.8 jit_solution(11264603741583361701)
XLA Ops:
  1.3 2.2 prep_low.3.refs_2_
  3.4 3.1 %collective-permute-start.5 = (bf16[2,192,640]{2,1,0:T(8,128)(2,1)}, bf16[2,192,640]{2,1,0:T(8,128)(2,1)S(1)}, u32[]{:S(2)}, u32[]{:S(2)}) collective-permute-start(bf16[2,192,640]{2,1,0:T(8,128)(2,1)} %prep_low.3.refs_2_), channel_id=1, source_target_pairs={{0,2},{1,3},{2,0},{3,1},{4,6},{5,7},{6,4},{7,5},{8,10},{9,11},{10,... | collective-permute-start | bytes 1474568 | tf_op jit(solution)/shard_map/ppermute | solution.py:601
  7.2 10.7 %collective-permute-done.5.refs_4_ = bf16[2,192,640]{2,1,0:T(8,128)(2,1)S(1)} collective-permute-done((bf16[2,192,640]{2,1,0:T(8,128)(2,1)}, bf16[2,192,640]{2,1,0:T(8,128)(2,1)S(1)}, u32[]{:S(2)}, u32[]{:S(2)}) %collective-permute-start.5) | collective-permute-done | bytes 491552 | tf_op jit(solution)/shard_map/ppermute | solution.py:601
  18.6 1.3 collective-permute-start.8
  19.9 1.3 collective-permute-start.11
  21.2 1.9 collective-permute-start.4
  23.1 2.2 prep_low.2.refs_2_
  25.3 13.6 %collective-permute-start = (bf16[2,192,640]{2,1,0:T(8,128)(2,1)}, bf16[2,192,640]{2,1,0:T(8,128)(2,1)}, u32[]{:S(2)}, u32[]{:S(2)}) collective-permute-start(bf16[2,192,640]{2,1,0:T(8,128)(2,1)} %prep_low.2.refs_2_), channel_id=1, source_target_pairs={{0,2},{1,3},{2,0},{3,1},{4,6},{5,7},{6,4},{7,5},{8,10},{9,11},{10,... | collective-permute-start | bytes 1474568 | tf_op jit(solution)/shard_map/ppermute | solution.py:601
  40.2 6.8 %collective-permute-done.11 = bf16[2,192,640]{2,1,0:T(8,128)(2,1)S(1)} collective-permute-done((bf16[2,192,640]{2,1,0:T(8,128)(2,1)S(1)}, bf16[2,192,640]{2,1,0:T(8,128)(2,1)S(1)}, u32[]{:S(2)}, u32[]{:S(2)}) %collective-permute-start.11) | collective-permute-done | bytes 491552 | tf_op jit(solution)/shard_map/ppermute | solution.py:601
  47.0 1.6 collective-permute-start.9
  49.2 6.5 %collective-permute-done.refs_4_ = bf16[2,192,640]{2,1,0:T(8,128)(2,1)} collective-permute-done((bf16[2,192,640]{2,1,0:T(8,128)(2,1)}, bf16[2,192,640]{2,1,0:T(8,128)(2,1)}, u32[]{:S(2)}, u32[]{:S(2)}) %collective-permute-start) | collective-permute-done | bytes 491552 | tf_op jit(solution)/shard_map/ppermute | solution.py:601
  56.4 1.3 collective-permute-start.3
  57.7 6.5 %collective-permute-done.9.refs_7_ = bf16[2,192,640]{2,1,0:T(8,128)(2,1)S(1)} collective-permute-done((bf16[2,192,640]{2,1,0:T(8,128)(2,1)S(1)}, bf16[2,192,640]{2,1,0:T(8,128)(2,1)S(1)}, u32[]{:S(2)}, u32[]{:S(2)}) %collective-permute-start.9) | collective-permute-done | bytes 491552 | tf_op jit(solution)/shard_map/ppermute | solution.py:601
  65.0 6.3 %collective-permute-done.12.refs_9_ = bf16[2,192,640]{2,1,0:T(8,128)(2,1)S(1)} collective-permute-done((bf16[2,192,640]{2,1,0:T(8,128)(2,1)S(1)}, bf16[2,192,640]{2,1,0:T(8,128)(2,1)S(1)}, u32[]{:S(2)}, u32[]{:S(2)}) %collective-permute-start.12) | collective-permute-done | bytes 491552 | tf_op jit(solution)/shard_map/ppermute | solution.py:601
  72.2 8.8 %product.2 = (f32[2,48,640]{2,1,0:T(8,128)}, f32[2,48,640]{2,1,0:T(8,128)}, f32[2,48,640]{2,1,0:T(8,128)}, f32[2,48,640]{2,1,0:T(8,128)}) custom-call(s32[6]{0:T(128)} %stack.27.pos_ref.refs_0_, bf16[2,2,320,2560]{3,2,1,0:T(8,128)(2,1)} %refs_1_.5, bf16[2,192,640]{2,1,0:T(8,128)(2,1)} %prep_low.3.refs_2_, ...), custom_call_target="tpu_custom_call" | custom-call | flops 2516582400 | bytes 10485760 | tf_op jit(solution)/shard_map/product/pallas_call | solution.py:286
  81.0 1.5 collective-permute-start.14
  82.9 2.7 %prep_shares.1 = (f32[2,48,640]{2,1,0:T(8,128)}, f32[2,48,640]{2,1,0:T(8,128)}, f32[2,48,640]{2,1,0:T(8,128)}, f32[2,48,640]{2,1,0:T(8,128)}, f32[1,128]{1,0:T(1,128)}) custom-call(s32[6]{0:T(128)} %stack.27.pos_ref.refs_0_, f32[2,2,192,320]{3,2,1,0:T(8,128)} %bitcast.22, f32[2,2,192,320]{3,2,1,0:T(8,128)} %bitcast.26), custom_call_target="tpu_custom_call" | custom-call | flops 737280 | bytes 2949120 | tf_op jit(solution)/shard_map/prep_shares/pallas_call | solution.py:197
  86.0 4.1 %collective-permute-done.14.refs_5_ = f32[2,48,640]{2,1,0:T(8,128)S(1)} collective-permute-done((f32[2,48,640]{2,1,0:T(8,128)}, f32[2,48,640]{2,1,0:T(8,128)S(1)}, u32[]{:S(2)}, u32[]{:S(2)}) %collective-permute-start.14) | collective-permute-done | bytes 245792 | tf_op jit(solution)/shard_map/ppermute | solution.py:580
  90.1 1.5 collective-permute-start.17
  91.6 2.9 %collective-permute-done.15.refs_6_ = f32[2,48,640]{2,1,0:T(8,128)S(1)} collective-permute-done((f32[2,48,640]{2,1,0:T(8,128)}, f32[2,48,640]{2,1,0:T(8,128)S(1)}, u32[]{:S(2)}, u32[]{:S(2)}) %collective-permute-start.15) | collective-permute-done | bytes 245792 | tf_op jit(solution)/shard_map/ppermute | solution.py:580
  94.5 1.8 collective-permute-start.18
  96.3 4.2 %gate_sum.1 = (f32[2,48,640]{2,1,0:T(8,128)}, f32[2,48,640]{2,1,0:T(8,128)}, f32[2,48,640]{2,1,0:T(8,128)}, f32[2,48,640]{2,1,0:T(8,128)}, f32[32,2,128]{2,1,0:T(2,128)}) custom-call(s32[6]{0:T(128)} %stack.27.pos_ref.refs_0_, s32[192,320]{1,0:T(8,128)} %bitcast.18, f32[1,128]{1,0:T(1,128)} %get-tuple-element.46.refs_2_, ...), custom_call_target="tpu_custom_call" | custom-call | flops 9830400 | bytes 1966080 | tf_op jit(solution)/shard_map/gate_sum/pallas_call | solution.py:460
  100.5 9.8 %all-to-all-start = ((f32[32,2,128]{2,1,0:T(2,128)}), f32[32,2,128]{2,1,0:T(2,128)S(1)}, u32[]{:S(2)}, u32[]{:S(2)}) async-start(f32[32,2,128]{2,1,0:T(2,128)} %get-tuple-element.51), calls=%async_computation | async-start | bytes 65536 | tf_op jit(solution)/shard_map/all_to_all | solution.py:626
  110.3 7.2 %all-to-all-done.refs_2_.refs_1_.t_ref = f32[32,2,128]{2,1,0:T(2,128)S(1)} async-done(((f32[32,2,128]{2,1,0:T(2,128)}), f32[32,2,128]{2,1,0:T(2,128)S(1)}, u32[]{:S(2)}, u32[]{:S(2)}) %all-to-all-start) | async-done | bytes 32800 | tf_op jit(solution)/shard_map/all_to_all | solution.py:626
  119.7 4.1 %gate.2 = (f32[2,48,640]{2,1,0:T(8,128)}, f32[2,48,640]{2,1,0:T(8,128)}, f32[2,48,640]{2,1,0:T(8,128)}, f32[2,48,640]{2,1,0:T(8,128)}) custom-call(s32[6]{0:T(128)} %stack.27.pos_ref.refs_0_, s32[192,320]{1,0:T(8,128)} %bitcast.19, f32[2,48,640]{2,1,0:T(8,128)} %get-tuple-element.53.refs_2_, f32[2,48,640]{2,1,0:T(8,128)} %copy-done.23, ...), custom_call_target="tpu_custom_call" | custom-call | flops 9830400 | bytes 1966080 | tf_op jit(solution)/shard_map/gate/pallas_call | solution.py:460
  123.8 4.7 %gate_mix.1 = (bf16[2,48,640]{2,1,0:T(8,128)(2,1)}, bf16[2,48,640]{2,1,0:T(8,128)(2,1)}, bf16[2,48,640]{2,1,0:T(8,128)(2,1)}, bf16[2,48,640]{2,1,0:T(8,128)(2,1)}) custom-call(s32[6]{0:T(128)} %stack.27.pos_ref.refs_0_, s32[192,320]{1,0:T(8,128)} %bitcast.20, f32[32,2,128]{2,1,0:T(2,128)} %copy-done.8, f32[2,48,640]{2,1,0:T(8,128)} %get-tuple-element.57.refs_3_, ...), custom_call_target="tpu_custom_call" | custom-call | flops 9830400 | bytes 1966080 | tf_op jit(solution)/shard_map/gate_mix/pallas_call | solution.py:460
  131.0 1.3 collective-permute-start.35
  132.4 2.6 %collective-permute-done.20.refs_3_ = bf16[2,48,640]{2,1,0:T(8,128)(2,1)S(1)} collective-permute-done((bf16[2,48,640]{2,1,0:T(8,128)(2,1)}, bf16[2,48,640]{2,1,0:T(8,128)(2,1)S(1)}, u32[]{:S(2)}, u32[]{:S(2)}) %collective-permute-start.20) | collective-permute-done | bytes 122912 | tf_op jit(solution)/shard_map/ppermute | solution.py:580
  135.0 1.5 collective-permute-done.21.refs_4_
  137.1 1.9 join.1.refs_2_
  139.0 2.7 %collective-permute-start.23 = (bf16[2,192,640]{2,1,0:T(8,128)(2,1)}, bf16[2,192,640]{2,1,0:T(8,128)(2,1)}, u32[]{:S(2)}, u32[]{:S(2)}) collective-permute-start(bf16[2,192,640]{2,1,0:T(8,128)(2,1)} %join.1.refs_2_), channel_id=1, source_target_pairs={{0,2},{1,3},{2,0},{3,1},{4,6},{5,7},{6,4},{7,5},{8,10},{9,11},{10,... | collective-permute-start | bytes 1474568 | tf_op jit(solution)/shard_map/ppermute | solution.py:601
  143.4 10.8 %collective-permute-done.23.refs_4_ = bf16[2,192,640]{2,1,0:T(8,128)(2,1)} collective-permute-done((bf16[2,192,640]{2,1,0:T(8,128)(2,1)}, bf16[2,192,640]{2,1,0:T(8,128)(2,1)}, u32[]{:S(2)}, u32[]{:S(2)}) %collective-permute-start.23) | collective-permute-done | bytes 491552 | tf_op jit(solution)/shard_map/ppermute | solution.py:601
  155.6 1.3 collective-permute-start.26
  156.9 1.4 collective-permute-start.22
  158.3 7.2 %collective-permute-done.36.refs_7_ = bf16[2,192,640]{2,1,0:T(8,128)(2,1)S(1)} collective-permute-done((bf16[2,192,640]{2,1,0:T(8,128)(2,1)S(1)}, bf16[2,192,640]{2,1,0:T(8,128)(2,1)S(1)}, u32[]{:S(2)}, u32[]{:S(2)}) %collective-permute-start.36) | collective-permute-done | bytes 491552 | tf_op jit(solution)/shard_map/ppermute | solution.py:601
  167.6 8.5 %collective-permute-done.38.refs_9_ = bf16[2,192,640]{2,1,0:T(8,128)(2,1)S(1)} collective-permute-done((bf16[2,192,640]{2,1,0:T(8,128)(2,1)S(1)}, bf16[2,192,640]{2,1,0:T(8,128)(2,1)S(1)}, u32[]{:S(2)}, u32[]{:S(2)}) %collective-permute-start.38) | collective-permute-done | bytes 491552 | tf_op jit(solution)/shard_map/ppermute | solution.py:601
  176.8 8.8 %product.3 = (f32[2,48,640]{2,1,0:T(8,128)}, f32[2,48,640]{2,1,0:T(8,128)}, f32[2,48,640]{2,1,0:T(8,128)}, f32[2,48,640]{2,1,0:T(8,128)}) custom-call(s32[6]{0:T(128)} %stack.27.pos_ref.refs_0_, bf16[2,2,320,2560]{3,2,1,0:T(8,128)(2,1)} %refs_1_.5, bf16[2,192,640]{2,1,0:T(8,128)(2,1)} %prep_low.2.refs_2_, ...), custom_call_target="tpu_custom_call" | custom-call | flops 2516582400 | bytes 10485760 | tf_op jit(solution)/shard_map/product/pallas_call | solution.py:286
  190.4 4.4 %collective-permute-done.40.refs_4_ = f32[2,48,640]{2,1,0:T(8,128)S(1)} collective-permute-done((f32[2,48,640]{2,1,0:T(8,128)}, f32[2,48,640]{2,1,0:T(8,128)S(1)}, u32[]{:S(2)}, u32[]{:S(2)}) %collective-permute-start.40) | collective-permute-done | bytes 245792 | tf_op jit(solution)/shard_map/ppermute | solution.py:580
  196.0 3.0 %collective-permute-done.41.refs_5_ = f32[2,48,640]{2,1,0:T(8,128)S(1)} collective-permute-done((f32[2,48,640]{2,1,0:T(8,128)S(1)}, f32[2,48,640]{2,1,0:T(8,128)S(1)}, u32[]{:S(2)}, u32[]{:S(2)}) %collective-permute-start.41) | collective-permute-done | bytes 245792 | tf_op jit(solution)/shard_map/ppermute | solution.py:580
  199.7 4.3 %gate.3 = (f32[2,48,640]{2,1,0:T(8,128)}, f32[2,48,640]{2,1,0:T(8,128)}, f32[2,48,640]{2,1,0:T(8,128)}, f32[2,48,640]{2,1,0:T(8,128)}) custom-call(s32[6]{0:T(128)} %stack.27.pos_ref.refs_0_, s32[192,320]{1,0:T(8,128)} %bitcast.21, f32[2,48,640]{2,1,0:T(8,128)} %get-tuple-element.72.refs_2_.refs_18_, f32[2,48,640]{2,1,0:T(8,128)} %copy-done.29, ...), custom_call_target="tpu_custom_call" | custom-call | flops 9830400 | bytes 1966080 | tf_op jit(solution)/shard_map/gate/pallas_call | solution.py:460
  204.8 1.4 collective-permute-start.33
  206.3 1.4 collective-permute-done.27.refs_7_
  208.3 9.3 %collective-permute-done.30.refs_9_ = bf16[2,192,640]{2,1,0:T(8,128)(2,1)S(1)} collective-permute-done((bf16[2,192,640]{2,1,0:T(8,128)(2,1)S(1)}, bf16[2,192,640]{2,1,0:T(8,128)(2,1)S(1)}, u32[]{:S(2)}, u32[]{:S(2)}) %collective-permute-start.30) | collective-permute-done | bytes 491552 | tf_op jit(solution)/shard_map/ppermute | solution.py:601
  218.4 8.4 %product_back.1 = (f32[2,2,192,320]{3,2,1,0:T(8,128)}, f32[1,128]{1,0:T(1,128)}) custom-call(s32[6]{0:T(128)} %stack.27.pos_ref.refs_0_, bf16[2,2,320,2560]{3,2,1,0:T(8,128)(2,1)} %refs_1_.5, bf16[2,192,640]{2,1,0:T(8,128)(2,1)} %join.1.refs_2_, bf16[2,192,640]{2,1,0:T(8,128)(2,1)} %collective-permute-done.22.refs_3_, ...), custom_call_target="tpu_custom_call" | custom-call | flops 2516582400 | bytes 10485760 | tf_op jit(solution)/shard_map/product_back/pallas_call | solution.py:286
  226.9 1.3 collective-permute-done.44.refs_13_
  228.8 6.1 %finish.1 = (f32[2,2,192,320]{3,2,1,0:T(8,128)}, f32[2,2,192,320]{3,2,1,0:T(8,128)}, f32[2,2,192,320]{3,2,1,0:T(8,128)}, f32[32,8,128]{2,1,0:T(8,128)}) custom-call(s32[6]{0:T(128)} %stack.27.pos_ref.refs_0_, f32[32,2,128]{2,1,0:T(2,128)} %copy-done.8, f32[2,2,192,320]{3,2,1,0:T(8,128)} %bitcast.23, f32[2,2,192,320]{3,2,1,0:T(8,128)} %bitcast.25, ...), custom_call_target="tpu_custom_call" | custom-call | flops 3440640 | bytes 9830400 | tf_op jit(solution)/shard_map/finish/pallas_call | solution.py:534
  234.9 11.7 %all_to_all.10.g_ref = f32[32,8,128]{2,1,0:T(8,128)} all-to-all(f32[32,8,128]{2,1,0:T(8,128)} %get-tuple-element.82), channel_id=1, replica_groups=mesh['freq'=4,'rcv'=8] {'freq','rcv'}, dimensions={0} | all-to-all | bytes 262144 | tf_op jit(solution)/shard_map/all_to_all | solution.py:626
  246.6 3.1 %turn.1 = (f32[2,2,192,320]{3,2,1,0:T(8,128)}, f32[2,2,192]{2,1,0:T(2,128)}) custom-call(s32[6]{0:T(128)} %stack.27.pos_ref.refs_0_, f32[32,2,128]{2,1,0:T(2,128)} %copy-done.8, f32[32,8,128]{2,1,0:T(8,128)} %all_to_all.10.g_ref, f32[2,2,192,320]{3,2,1,0:T(8,128)} %get-tuple-element.83.new_ref, f32[2,2,192,320]{3,2,1,0:T(8,128)} %bitcast.17), custom_call_target="tpu_custom_call" | custom-call | flops 491520 | bytes 2949120 | tf_op jit(solution)/shard_map/turn/pallas_call | solution.py:563
  (141 shorter events, 27.6 us)
Async XLA Ops:
  3.4 14.5 %collective-permute-start.5 = (bf16[2,192,640]{2,1,0:T(8,128)(2,1)}, bf16[2,192,640]{2,1,0:T(8,128)(2,1)S(1)}, u32[]{:S(2)}, u32[]{:S(2)}) collective-permute-start(bf16[2,192,640]{2,1,0:T(8,128)(2,1)} %prep_low.3.refs_2_), channel_id=1, source_target_pairs={{0,2},{1,3},{2,0},{3,1},{4,6},{5,7},{6,4},{7,5},{8,10},{9,11},{10,... | collective-permute-start | bytes 1474568 | tf_op jit(solution)/shard_map/ppermute | solution.py:601
  6.5 12.1 %collective-permute-start.7 = (bf16[2,192,640]{2,1,0:T(8,128)(2,1)}, bf16[2,192,640]{2,1,0:T(8,128)(2,1)S(1)}, u32[]{:S(2)}, u32[]{:S(2)}) collective-permute-start(bf16[2,192,640]{2,1,0:T(8,128)(2,1)} %prep_low.3.refs_2_), channel_id=1, source_target_pairs={{2,4},{3,5},{4,2},{5,3},{10,12},{11,13},{12,10},{13,11},{18,20},{1... | collective-permute-start | bytes 1474568 | tf_op jit(solution)/shard_map/ppermute | solution.py:601
  17.9 2.0 collective-permute-start.10
  18.6 20.9 %collective-permute-start.8 = (bf16[2,192,640]{2,1,0:T(8,128)(2,1)S(1)}, bf16[2,192,640]{2,1,0:T(8,128)(2,1)S(1)}, u32[]{:S(2)}, u32[]{:S(2)}) collective-permute-start(bf16[2,192,640]{2,1,0:T(8,128)(2,1)S(1)} %collective-permute-done.7), channel_id=1, source_target_pairs={{2,0},{3,1},{4,6},{5,7},{10,8},{11,9},{12,14},{13,15},{18,16},{19,... | collective-permute-start | bytes 1474568 | tf_op jit(solution)/shard_map/ppermute | solution.py:601
  19.9 27.1 %collective-permute-start.11 = (bf16[2,192,640]{2,1,0:T(8,128)(2,1)S(1)}, bf16[2,192,640]{2,1,0:T(8,128)(2,1)S(1)}, u32[]{:S(2)}, u32[]{:S(2)}) collective-permute-start(bf16[2,192,640]{2,1,0:T(8,128)(2,1)S(1)} %collective-permute-done.10), channel_id=1, source_target_pairs={{2,0},{3,1},{4,6},{5,7},{10,8},{11,9},{12,14},{13,15},{18,16},{19,... | collective-permute-start | bytes 1474568 | tf_op jit(solution)/shard_map/ppermute | solution.py:601
  21.2 27.5 %collective-permute-start.4 = (bf16[2,192,640]{2,1,0:T(8,128)(2,1)}, bf16[2,192,640]{2,1,0:T(8,128)(2,1)}, u32[]{:S(2)}, u32[]{:S(2)}) collective-permute-start(bf16[2,192,640]{2,1,0:T(8,128)(2,1)} %prep_low.3.refs_2_), channel_id=1, source_target_pairs={{0,1},{1,0},{2,3},{3,2},{4,5},{5,4},{6,7},{7,6},{8,9},{9,8},{10,11... | collective-permute-start | bytes 1474568 | tf_op jit(solution)/shard_map/ppermute | solution.py:601
  25.3 30.4 %collective-permute-start = (bf16[2,192,640]{2,1,0:T(8,128)(2,1)}, bf16[2,192,640]{2,1,0:T(8,128)(2,1)}, u32[]{:S(2)}, u32[]{:S(2)}) collective-permute-start(bf16[2,192,640]{2,1,0:T(8,128)(2,1)} %prep_low.2.refs_2_), channel_id=1, source_target_pairs={{0,2},{1,3},{2,0},{3,1},{4,6},{5,7},{6,4},{7,5},{8,10},{9,11},{10,... | collective-permute-start | bytes 1474568 | tf_op jit(solution)/shard_map/ppermute | solution.py:601
  38.8 17.5 %collective-permute-start.2 = (bf16[2,192,640]{2,1,0:T(8,128)(2,1)}, bf16[2,192,640]{2,1,0:T(8,128)(2,1)S(1)}, u32[]{:S(2)}, u32[]{:S(2)}) collective-permute-start(bf16[2,192,640]{2,1,0:T(8,128)(2,1)} %prep_low.2.refs_2_), channel_id=1, source_target_pairs={{2,4},{3,5},{4,2},{5,3},{10,12},{11,13},{12,10},{13,11},{18,20},{1... | collective-permute-start | bytes 1474568 | tf_op jit(solution)/shard_map/ppermute | solution.py:601
  39.6 18.1 %collective-permute-start.6 = (bf16[2,192,640]{2,1,0:T(8,128)(2,1)S(1)}, bf16[2,192,640]{2,1,0:T(8,128)(2,1)S(1)}, u32[]{:S(2)}, u32[]{:S(2)}) collective-permute-start(bf16[2,192,640]{2,1,0:T(8,128)(2,1)S(1)} %collective-permute-done.5.refs_4_), channel_id=1, source_target_pairs={{0,1},{1,0},{2,3},{3,2},{4,5},{5,4},{6,7},{7,6},{8,9},{9,8},{10,11... | collective-permute-start | bytes 1474568 | tf_op jit(solution)/shard_map/ppermute | solution.py:601
  47.0 17.3 %collective-permute-start.9 = (bf16[2,192,640]{2,1,0:T(8,128)(2,1)S(1)}, bf16[2,192,640]{2,1,0:T(8,128)(2,1)S(1)}, u32[]{:S(2)}, u32[]{:S(2)}) collective-permute-start(bf16[2,192,640]{2,1,0:T(8,128)(2,1)S(1)} %broadcast_select_fusion.5.refs_6_), channel_id=1, source_target_pairs={{0,1},{1,0},{2,3},{3,2},{4,5},{5,4},{6,7},{7,6},{8,9},{9,8},{10,11... | collective-permute-start | bytes 1474568 | tf_op jit(solution)/shard_map/ppermute | solution.py:601
  48.7 22.7 %collective-permute-start.12 = (bf16[2,192,640]{2,1,0:T(8,128)(2,1)S(1)}, bf16[2,192,640]{2,1,0:T(8,128)(2,1)S(1)}, u32[]{:S(2)}, u32[]{:S(2)}) collective-permute-start(bf16[2,192,640]{2,1,0:T(8,128)(2,1)S(1)} %broadcast_select_fusion.4.refs_8_), channel_id=1, source_target_pairs={{0,1},{1,0},{2,3},{3,2},{4,5},{5,4},{6,7},{7,6},{8,9},{9,8},{10,11... | collective-permute-start | bytes 1474568 | tf_op jit(solution)/shard_map/ppermute | solution.py:601
  55.7 54.6 %collective-permute-start.1 = (bf16[2,192,640]{2,1,0:T(8,128)(2,1)}, bf16[2,192,640]{2,1,0:T(8,128)(2,1)S(1)}, u32[]{:S(2)}, u32[]{:S(2)}) collective-permute-start(bf16[2,192,640]{2,1,0:T(8,128)(2,1)} %collective-permute-done.refs_4_), channel_id=1, source_target_pairs={{2,4},{3,5},{4,2},{5,3},{10,12},{11,13},{12,10},{13,11},{18,20},{1... | collective-permute-start | bytes 1474568 | tf_op jit(solution)/shard_map/ppermute | solution.py:601
  56.4 53.9 %collective-permute-start.3 = (bf16[2,192,640]{2,1,0:T(8,128)(2,1)S(1)}, bf16[2,192,640]{2,1,0:T(8,128)(2,1)S(1)}, u32[]{:S(2)}, u32[]{:S(2)}) collective-permute-start(bf16[2,192,640]{2,1,0:T(8,128)(2,1)S(1)} %collective-permute-done.2), channel_id=1, source_target_pairs={{2,0},{3,1},{4,6},{5,7},{10,8},{11,9},{12,14},{13,15},{18,16},{19,... | collective-permute-start | bytes 1474568 | tf_op jit(solution)/shard_map/ppermute | solution.py:601
  81.0 4.7 %collective-permute-start.13 = (f32[2,48,640]{2,1,0:T(8,128)}, f32[2,48,640]{2,1,0:T(8,128)S(1)}, u32[]{:S(2)}, u32[]{:S(2)}) collective-permute-start(f32[2,48,640]{2,1,0:T(8,128)} %get-tuple-element.48.refs_15_), channel_id=1, source_target_pairs={{0,8},{8,0},{16,24},{24,16},{1,9},{9,1},{17,25},{25,17},{2,10},{10... | collective-permute-start | bytes 737288 | tf_op jit(solution)/shard_map/ppermute | solution.py:580
  81.0 9.1 %collective-permute-start.14 = (f32[2,48,640]{2,1,0:T(8,128)}, f32[2,48,640]{2,1,0:T(8,128)S(1)}, u32[]{:S(2)}, u32[]{:S(2)}) collective-permute-start(f32[2,48,640]{2,1,0:T(8,128)} %get-tuple-element.49.refs_16_), channel_id=1, source_target_pairs={{0,16},{8,24},{16,0},{24,8},{1,17},{9,25},{17,1},{25,9},{2,18},{10... | collective-permute-start | bytes 737288 | tf_op jit(solution)/shard_map/ppermute | solution.py:580
  82.6 11.9 %collective-permute-start.15 = (f32[2,48,640]{2,1,0:T(8,128)}, f32[2,48,640]{2,1,0:T(8,128)S(1)}, u32[]{:S(2)}, u32[]{:S(2)}) collective-permute-start(f32[2,48,640]{2,1,0:T(8,128)} %get-tuple-element.50.refs_17_), channel_id=1, source_target_pairs={{0,24},{8,16},{16,8},{24,0},{1,25},{9,17},{17,9},{25,1},{2,26},{10... | collective-permute-start | bytes 737288 | tf_op jit(solution)/shard_map/ppermute | solution.py:580
  85.6 33.2 %collective-permute-start.16 = (f32[2,48,640]{2,1,0:T(8,128)}, f32[2,48,640]{2,1,0:T(8,128)S(1)}, u32[]{:S(2)}, u32[]{:S(2)}) collective-permute-start(f32[2,48,640]{2,1,0:T(8,128)} %get-tuple-element.54), channel_id=1, source_target_pairs={{0,8},{8,0},{16,24},{24,16},{1,9},{9,1},{17,25},{25,17},{2,10},{10... | collective-permute-start | bytes 737288 | tf_op jit(solution)/shard_map/ppermute | solution.py:580
  90.1 28.7 %collective-permute-start.17 = (f32[2,48,640]{2,1,0:T(8,128)}, f32[2,48,640]{2,1,0:T(8,128)S(1)}, u32[]{:S(2)}, u32[]{:S(2)}) collective-permute-start(f32[2,48,640]{2,1,0:T(8,128)} %get-tuple-element.55), channel_id=1, source_target_pairs={{0,16},{8,24},{16,0},{24,8},{1,17},{9,25},{17,1},{25,9},{2,18},{10... | collective-permute-start | bytes 737288 | tf_op jit(solution)/shard_map/ppermute | solution.py:580
  94.5 24.3 %collective-permute-start.18 = (f32[2,48,640]{2,1,0:T(8,128)}, f32[2,48,640]{2,1,0:T(8,128)S(1)}, u32[]{:S(2)}, u32[]{:S(2)}) collective-permute-start(f32[2,48,640]{2,1,0:T(8,128)} %get-tuple-element.56), channel_id=1, source_target_pairs={{0,24},{8,16},{16,8},{24,0},{1,25},{9,17},{17,9},{25,1},{2,26},{10... | collective-permute-start | bytes 737288 | tf_op jit(solution)/shard_map/ppermute | solution.py:580
  100.5 17.0 %all-to-all-start = ((f32[32,2,128]{2,1,0:T(2,128)}), f32[32,2,128]{2,1,0:T(2,128)S(1)}, u32[]{:S(2)}, u32[]{:S(2)}) async-start(f32[32,2,128]{2,1,0:T(2,128)} %get-tuple-element.51), calls=%async_computation | async-start | bytes 65536 | tf_op jit(solution)/shard_map/all_to_all | solution.py:626
  117.5 25.1 %collective-permute-start.37 = (bf16[2,192,640]{2,1,0:T(8,128)(2,1)S(1)}, bf16[2,192,640]{2,1,0:T(8,128)(2,1)S(1)}, u32[]{:S(2)}, u32[]{:S(2)}) collective-permute-start(bf16[2,192,640]{2,1,0:T(8,128)(2,1)S(1)} %collective-permute-done.1), channel_id=1, source_target_pairs={{2,0},{3,1},{4,6},{5,7},{10,8},{11,9},{12,14},{13,15},{18,16},{19,... | collective-permute-start | bytes 1474568 | tf_op jit(solution)/shard_map/ppermute | solution.py:601
  128.5 2.6 %collective-permute-start.19 = (bf16[2,48,640]{2,1,0:T(8,128)(2,1)}, bf16[2,48,640]{2,1,0:T(8,128)(2,1)S(1)}, u32[]{:S(2)}, u32[]{:S(2)}) collective-permute-start(bf16[2,48,640]{2,1,0:T(8,128)(2,1)} %get-tuple-element.66), channel_id=1, source_target_pairs={{0,8},{8,0},{16,24},{24,16},{1,9},{9,1},{17,25},{25,17},{2,10},{10... | collective-permute-start | bytes 368648 | tf_op jit(solution)/shard_map/ppermute | solution.py:580
  128.6 6.4 %collective-permute-start.20 = (bf16[2,48,640]{2,1,0:T(8,128)(2,1)}, bf16[2,48,640]{2,1,0:T(8,128)(2,1)S(1)}, u32[]{:S(2)}, u32[]{:S(2)}) collective-permute-start(bf16[2,48,640]{2,1,0:T(8,128)(2,1)} %get-tuple-element.67), channel_id=1, source_target_pairs={{0,16},{8,24},{16,0},{24,8},{1,17},{9,25},{17,1},{25,9},{2,18},{10... | collective-permute-start | bytes 368648 | tf_op jit(solution)/shard_map/ppermute | solution.py:580
  129.2 7.3 %collective-permute-start.21 = (bf16[2,48,640]{2,1,0:T(8,128)(2,1)}, bf16[2,48,640]{2,1,0:T(8,128)(2,1)S(1)}, u32[]{:S(2)}, u32[]{:S(2)}) collective-permute-start(bf16[2,48,640]{2,1,0:T(8,128)(2,1)} %get-tuple-element.68), channel_id=1, source_target_pairs={{0,24},{8,16},{16,8},{24,0},{1,25},{9,17},{17,9},{25,1},{2,26},{10... | collective-permute-start | bytes 368648 | tf_op jit(solution)/shard_map/ppermute | solution.py:580
  130.3 24.5 %collective-permute-start.34 = (bf16[2,192,640]{2,1,0:T(8,128)(2,1)S(1)}, bf16[2,192,640]{2,1,0:T(8,128)(2,1)}, u32[]{:S(2)}, u32[]{:S(2)}) collective-permute-start(bf16[2,192,640]{2,1,0:T(8,128)(2,1)S(1)} %copy-done.1), channel_id=1, source_target_pairs={{0,1},{1,0},{2,3},{3,2},{4,5},{5,4},{6,7},{7,6},{8,9},{9,8},{10,11... | collective-permute-start | bytes 1474568 | tf_op jit(solution)/shard_map/ppermute | solution.py:601
  131.0 25.9 %collective-permute-start.35 = (bf16[2,192,640]{2,1,0:T(8,128)(2,1)}, bf16[2,192,640]{2,1,0:T(8,128)(2,1)}, u32[]{:S(2)}, u32[]{:S(2)}) collective-permute-start(bf16[2,192,640]{2,1,0:T(8,128)(2,1)} %collective-permute-done.refs_4_), channel_id=1, source_target_pairs={{0,1},{1,0},{2,3},{3,2},{4,5},{5,4},{6,7},{7,6},{8,9},{9,8},{10,11... | collective-permute-start | bytes 1474568 | tf_op jit(solution)/shard_map/ppermute | solution.py:601
  139.0 15.1 %collective-permute-start.23 = (bf16[2,192,640]{2,1,0:T(8,128)(2,1)}, bf16[2,192,640]{2,1,0:T(8,128)(2,1)}, u32[]{:S(2)}, u32[]{:S(2)}) collective-permute-start(bf16[2,192,640]{2,1,0:T(8,128)(2,1)} %join.1.refs_2_), channel_id=1, source_target_pairs={{0,2},{1,3},{2,0},{3,1},{4,6},{5,7},{6,4},{7,5},{8,10},{9,11},{10,... | collective-permute-start | bytes 1474568 | tf_op jit(solution)/shard_map/ppermute | solution.py:601
  141.8 34.2 %copy-start.4 = (bf16[2,192,640]{2,1,0:T(8,128)(2,1)}, bf16[2,192,640]{2,1,0:T(8,128)(2,1)S(1)}, u32[]{:S(2)}) copy-start(bf16[2,192,640]{2,1,0:T(8,128)(2,1)S(1)} %broadcast_select_fusion.1.refs_6_) | copy-start | bytes 1474564
  141.8 23.7 %collective-permute-start.36 = (bf16[2,192,640]{2,1,0:T(8,128)(2,1)S(1)}, bf16[2,192,640]{2,1,0:T(8,128)(2,1)S(1)}, u32[]{:S(2)}, u32[]{:S(2)}) collective-permute-start(bf16[2,192,640]{2,1,0:T(8,128)(2,1)S(1)} %broadcast_select_fusion.1.refs_6_), channel_id=1, source_target_pairs={{0,1},{1,0},{2,3},{3,2},{4,5},{5,4},{6,7},{7,6},{8,9},{9,8},{10,11... | collective-permute-start | bytes 1474568 | tf_op jit(solution)/shard_map/ppermute | solution.py:601
  142.6 13.0 %collective-permute-start.25 = (bf16[2,192,640]{2,1,0:T(8,128)(2,1)S(1)}, bf16[2,192,640]{2,1,0:T(8,128)(2,1)S(1)}, u32[]{:S(2)}, u32[]{:S(2)}) collective-permute-start(bf16[2,192,640]{2,1,0:T(8,128)(2,1)S(1)} %copy-done), channel_id=1, source_target_pairs={{2,4},{3,5},{4,2},{5,3},{10,12},{11,13},{12,10},{13,11},{18,20},{1... | collective-permute-start | bytes 1474568 | tf_op jit(solution)/shard_map/ppermute | solution.py:601
  143.4 32.7 %copy-start.5 = (bf16[2,192,640]{2,1,0:T(8,128)(2,1)}, bf16[2,192,640]{2,1,0:T(8,128)(2,1)S(1)}, u32[]{:S(2)}) copy-start(bf16[2,192,640]{2,1,0:T(8,128)(2,1)S(1)} %broadcast_select_fusion.refs_8_) | copy-start | bytes 1474564
  154.2 12.1 %collective-permute-start.28 = (bf16[2,192,640]{2,1,0:T(8,128)(2,1)}, bf16[2,192,640]{2,1,0:T(8,128)(2,1)S(1)}, u32[]{:S(2)}, u32[]{:S(2)}) collective-permute-start(bf16[2,192,640]{2,1,0:T(8,128)(2,1)} %collective-permute-done.23.refs_4_), channel_id=1, source_target_pairs={{2,4},{3,5},{4,2},{5,3},{10,12},{11,13},{12,10},{13,11},{18,20},{1... | collective-permute-start | bytes 1474568 | tf_op jit(solution)/shard_map/ppermute | solution.py:601
  154.8 21.2 %collective-permute-start.38 = (bf16[2,192,640]{2,1,0:T(8,128)(2,1)S(1)}, bf16[2,192,640]{2,1,0:T(8,128)(2,1)S(1)}, u32[]{:S(2)}, u32[]{:S(2)}) collective-permute-start(bf16[2,192,640]{2,1,0:T(8,128)(2,1)S(1)} %broadcast_select_fusion.refs_8_), channel_id=1, source_target_pairs={{0,1},{1,0},{2,3},{3,2},{4,5},{5,4},{6,7},{7,6},{8,9},{9,8},{10,11... | collective-permute-start | bytes 1474568 | tf_op jit(solution)/shard_map/ppermute | solution.py:601
  155.6 30.1 %collective-permute-start.26 = (bf16[2,192,640]{2,1,0:T(8,128)(2,1)S(1)}, bf16[2,192,640]{2,1,0:T(8,128)(2,1)S(1)}, u32[]{:S(2)}, u32[]{:S(2)}) collective-permute-start(bf16[2,192,640]{2,1,0:T(8,128)(2,1)S(1)} %collective-permute-done.25), channel_id=1, source_target_pairs={{2,0},{3,1},{4,6},{5,7},{10,8},{11,9},{12,14},{13,15},{18,16},{19,... | collective-permute-start | bytes 1474568 | tf_op jit(solution)/shard_map/ppermute | solution.py:601
  156.9 47.8 %collective-permute-start.22 = (bf16[2,192,640]{2,1,0:T(8,128)(2,1)S(1)}, bf16[2,192,640]{2,1,0:T(8,128)(2,1)}, u32[]{:S(2)}, u32[]{:S(2)}) collective-permute-start(bf16[2,192,640]{2,1,0:T(8,128)(2,1)S(1)} %copy-done), channel_id=1, source_target_pairs={{0,1},{1,0},{2,3},{3,2},{4,5},{5,4},{6,7},{7,6},{8,9},{9,8},{10,11... | collective-permute-start | bytes 1474568 | tf_op jit(solution)/shard_map/ppermute | solution.py:601
  165.5 40.7 %collective-permute-start.24 = (bf16[2,192,640]{2,1,0:T(8,128)(2,1)}, bf16[2,192,640]{2,1,0:T(8,128)(2,1)}, u32[]{:S(2)}, u32[]{:S(2)}) collective-permute-start(bf16[2,192,640]{2,1,0:T(8,128)(2,1)} %collective-permute-done.23.refs_4_), channel_id=1, source_target_pairs={{0,1},{1,0},{2,3},{3,2},{4,5},{5,4},{6,7},{7,6},{8,9},{9,8},{10,11... | collective-permute-start | bytes 1474568 | tf_op jit(solution)/shard_map/ppermute | solution.py:601
  166.3 21.6 %collective-permute-start.29 = (bf16[2,192,640]{2,1,0:T(8,128)(2,1)S(1)}, bf16[2,192,640]{2,1,0:T(8,128)(2,1)}, u32[]{:S(2)}, u32[]{:S(2)}) collective-permute-start(bf16[2,192,640]{2,1,0:T(8,128)(2,1)S(1)} %collective-permute-done.28), channel_id=1, source_target_pairs={{2,0},{3,1},{4,6},{5,7},{10,8},{11,9},{12,14},{13,15},{18,16},{19,... | collective-permute-start | bytes 1474568 | tf_op jit(solution)/shard_map/ppermute | solution.py:601
  185.7 1.8 collective-permute-start.39
  185.8 9.1 %collective-permute-start.40 = (f32[2,48,640]{2,1,0:T(8,128)}, f32[2,48,640]{2,1,0:T(8,128)S(1)}, u32[]{:S(2)}, u32[]{:S(2)}) collective-permute-start(f32[2,48,640]{2,1,0:T(8,128)} %get-tuple-element.74.refs_20_), channel_id=1, source_target_pairs={{0,16},{8,24},{16,0},{24,8},{1,17},{9,25},{17,1},{25,9},{2,18},{10... | collective-permute-start | bytes 737288 | tf_op jit(solution)/shard_map/ppermute | solution.py:580
  187.5 11.6 %collective-permute-start.41 = (f32[2,48,640]{2,1,0:T(8,128)S(1)}, f32[2,48,640]{2,1,0:T(8,128)S(1)}, u32[]{:S(2)}, u32[]{:S(2)}) collective-permute-start(f32[2,48,640]{2,1,0:T(8,128)S(1)} %copy-done.19), channel_id=1, source_target_pairs={{0,24},{8,16},{16,8},{24,0},{1,25},{9,17},{17,9},{25,1},{2,26},{10... | collective-permute-start | bytes 737288 | tf_op jit(solution)/shard_map/ppermute | solution.py:580
  188.1 19.5 %collective-permute-start.27 = (bf16[2,192,640]{2,1,0:T(8,128)(2,1)S(1)}, bf16[2,192,640]{2,1,0:T(8,128)(2,1)S(1)}, u32[]{:S(2)}, u32[]{:S(2)}) collective-permute-start(bf16[2,192,640]{2,1,0:T(8,128)(2,1)S(1)} %broadcast_select_fusion.3.refs_6_), channel_id=1, source_target_pairs={{0,1},{1,0},{2,3},{3,2},{4,5},{5,4},{6,7},{7,6},{8,9},{9,8},{10,11... | collective-permute-start | bytes 1474568 | tf_op jit(solution)/shard_map/ppermute | solution.py:601
  194.9 22.7 %collective-permute-start.30 = (bf16[2,192,640]{2,1,0:T(8,128)(2,1)S(1)}, bf16[2,192,640]{2,1,0:T(8,128)(2,1)S(1)}, u32[]{:S(2)}, u32[]{:S(2)}) collective-permute-start(bf16[2,192,640]{2,1,0:T(8,128)(2,1)S(1)} %broadcast_select_fusion.2.refs_8_), channel_id=1, source_target_pairs={{0,1},{1,0},{2,3},{3,2},{4,5},{5,4},{6,7},{7,6},{8,9},{9,8},{10,11... | collective-permute-start | bytes 1474568 | tf_op jit(solution)/shard_map/ppermute | solution.py:601
  199.0 5.0 %collective-permute-start.31 = (f32[2,48,640]{2,1,0:T(8,128)}, f32[2,48,640]{2,1,0:T(8,128)S(1)}, u32[]{:S(2)}, u32[]{:S(2)}) collective-permute-start(f32[2,48,640]{2,1,0:T(8,128)} %get-tuple-element.62.refs_8_), channel_id=1, source_target_pairs={{0,8},{8,0},{16,24},{24,16},{1,9},{9,1},{17,25},{25,17},{2,10},{10... | collective-permute-start | bytes 737288 | tf_op jit(solution)/shard_map/ppermute | solution.py:580
  204.1 22.7 %collective-permute-start.32 = (f32[2,48,640]{2,1,0:T(8,128)S(1)}, f32[2,48,640]{2,1,0:T(8,128)S(1)}, u32[]{:S(2)}, u32[]{:S(2)}) collective-permute-start(f32[2,48,640]{2,1,0:T(8,128)S(1)} %copy-done.18), channel_id=1, source_target_pairs={{0,16},{8,24},{16,0},{24,8},{1,17},{9,25},{17,1},{25,9},{2,18},{10... | collective-permute-start | bytes 737288 | tf_op jit(solution)/shard_map/ppermute | solution.py:580
  204.8 22.0 %collective-permute-start.33 = (f32[2,48,640]{2,1,0:T(8,128)S(1)}, f32[2,48,640]{2,1,0:T(8,128)S(1)}, u32[]{:S(2)}, u32[]{:S(2)}) collective-permute-start(f32[2,48,640]{2,1,0:T(8,128)S(1)} %copy-done.17), channel_id=1, source_target_pairs={{0,24},{8,16},{16,8},{24,0},{1,25},{9,17},{17,9},{25,1},{2,26},{10... | collective-permute-start | bytes 737288 | tf_op jit(solution)/shard_map/ppermute | solution.py:580
  206.1 20.7 %collective-permute-start.42 = (f32[2,48,640]{2,1,0:T(8,128)}, f32[2,48,640]{2,1,0:T(8,128)S(1)}, u32[]{:S(2)}, u32[]{:S(2)}) collective-permute-start(f32[2,48,640]{2,1,0:T(8,128)} %get-tuple-element.77), channel_id=1, source_target_pairs={{0,8},{8,0},{16,24},{24,16},{1,9},{9,1},{17,25},{25,17},{2,10},{10... | collective-permute-start | bytes 737288 | tf_op jit(solution)/shard_map/ppermute | solution.py:580
  207.6 19.2 %collective-permute-start.43 = (f32[2,48,640]{2,1,0:T(8,128)}, f32[2,48,640]{2,1,0:T(8,128)S(1)}, u32[]{:S(2)}, u32[]{:S(2)}) collective-permute-start(f32[2,48,640]{2,1,0:T(8,128)} %get-tuple-element.78), channel_id=1, source_target_pairs={{0,16},{8,24},{16,0},{24,8},{1,17},{9,25},{17,1},{25,9},{2,18},{10... | collective-permute-start | bytes 737288 | tf_op jit(solution)/shard_map/ppermute | solution.py:580
  217.6 10.5 %collective-permute-start.44 = (f32[2,48,640]{2,1,0:T(8,128)}, f32[2,48,640]{2,1,0:T(8,128)S(1)}, u32[]{:S(2)}, u32[]{:S(2)}) collective-permute-start(f32[2,48,640]{2,1,0:T(8,128)} %get-tuple-element.79), channel_id=1, source_target_pairs={{0,24},{8,16},{16,8},{24,0},{1,25},{9,17},{17,9},{25,1},{2,26},{10... | collective-permute-start | bytes 737288 | tf_op jit(solution)/shard_map/ppermute | solution.py:580
  (36 other events, 256.3 us)
where the time goes:
time: 251 us; the launch traced here: 250 us
  waiting for transfers between devices  102 us (41%)
  starting transfers between devices  65.7 us (26%)
  Pallas kernels  61.5 us (25%)
  blocking collectives  11.7 us (5%)
  local copies, waits for them, and re-layouts  6.34 us (3%)
    ppermute x27, waiting for transfers between devices, move(): return lax.ppermute(v, 'rcv', pairs)  74.1 us
    ppermute x27, starting transfers between devices, move(): return lax.ppermute(v, 'rcv', pairs)  43.7 us
    pallas_call x3, Pallas kernels, product(): pl.pallas_call(lambda *refs: product_kernel(groups, count, back, *refs),...  26 us
    ppermute x18, waiting for transfers between devices, exchange(): out.append(lax.ppermute(shares[p], 'freq', pairs))  20.8 us
    pallas_call x4, Pallas kernels, gate(): pl.pallas_call(lambda *refs: gate_kernel(groups, squares, bool(bases), *r...  17.3 us
    ppermute x18, starting transfers between devices, exchange(): out.append(lax.ppermute(shares[p], 'freq', pairs))  12.2 us
    all_to_all x1, blocking collectives, total_over_all(): lax.all_to_all(sent, ('freq', 'rcv'), split_axis=0, concat_axis=0, tiled=...  11.7 us
    all_to_all x1, starting transfers between devices, total_over_all(): lax.all_to_all(sent, ('freq', 'rcv'), split_axis=0, concat_axis=0, tiled=...  9.8 us
  transfers between devices with their start and end apart: 46, of which 19 were waited for; matrix products, arithmetic and copies ran while one was open for 1% of the time, Pallas kernels for 20%

commit v1 on v0

--- a/solution.py
+++ b/solution.py
@@ -18,9 +18,11 @@
 COSINE = [(-1.0) ** i / math.factorial(2 * i) for i in range(8)]
 
 
+LIMIT = 20 * 2**20
+
 VMEM = pl.BlockSpec(memory_space=pltpu.VMEM)
 SMEM = pl.BlockSpec(memory_space=pltpu.SMEM)
-ANY = pl.BlockSpec(memory_space=pl.ANY)
+GRANT = pltpu.CompilerParams(vmem_limit_bytes=LIMIT)
 
 
 def tables(count):
@@ -154,6 +156,7 @@
         in_specs=[SMEM, VMEM],
         out_specs=VMEM,
         cost_estimate=cost(x.size, 6 * x.size),
+        compiler_params=GRANT,
         name="prep_low",
     )(pos, x)
 
@@ -200,19 +203,20 @@
         in_specs=[SMEM, VMEM, VMEM],
         out_specs=[VMEM] * (groups + 1),
         cost_estimate=cost(3 * x.size, 12 * x.size),
+        compiler_params=GRANT,
         name="prep_shares",
     )(pos, x, g)
 
 
-def product_kernel(groups, count, conjugate, pos_ref, r_ref, *refs):
+def product_kernel(groups, count, back, pos_ref, r_ref, *refs):
     blocks, refs = refs[: 2 * count], refs[2 * count :]
     v_scr, acc = refs[-2:]
-    f = pl.program_id(0)
-    _, kc, wide = blocks[0].shape
+    loc, kc, wide = blocks[0].shape
     rows = r_ref.shape[2]
     main = wide // 2 - HALF
-
-    def load(odd):
+    me = pos_ref[0]
+
+    def load(f, odd):
         for b in range(count):
             even = blocks[2 * b + odd]
             other = blocks[2 * b + 1 - odd]
@@ -221,86 +225,61 @@
                 here = slice(c * kc, (c + 1) * kc)
                 half = slice(2 * main + c * HALF, 2 * main + (c + 1) * HALF)
                 lanes = lambda shift, size: pl.ds(pl.multiple_of(at + shift, LANES), size)
-                v_scr[here, lanes(0, main)] = even[0, :, c * main : (c + 1) * main]
-                middle = [even[0, :, half], other[0, :, half]]
+                v_scr[here, lanes(0, main)] = even[f, :, c * main : (c + 1) * main]
+                middle = [even[f, :, half], other[f, :, half]]
                 v_scr[here, lanes(main, LANES)] = jnp.concatenate(middle, axis=1)
-                v_scr[here, lanes(main + LANES, main)] = other[0, :, c * main : (c + 1) * main]
-
-    by_parity(pos_ref, load)
-    both = r_ref[0].reshape(2 * rows, r_ref.shape[3])
+                v_scr[here, lanes(main + LANES, main)] = other[f, :, c * main : (c + 1) * main]
+
+    def shares(f, odd):
+        ks = kc // groups
+        for p in range(groups):
+            at = pl.multiple_of(share_of(me, p, groups) * ks, ks)
+            real = acc[pl.ds(at, ks), :rows] - acc[pl.ds(at + kc, ks), rows:]
+            imag = acc[pl.ds(at + kc, ks), :rows] + acc[pl.ds(at, ks), rows:]
+            refs[p][f] = pack(real, imag, odd)
+
     dims = (((1,), (1,)), ((), ()))
-    acc[...] = lax.dot_general(v_scr[...], both, dims, preferred_element_type=jnp.float32)
-    if not conjugate:
-        me = pos_ref[0]
-        ks = kc // groups
-
-        def finish(odd):
-            for p in range(groups):
-                at = pl.multiple_of(share_of(me, p, groups) * ks, ks)
-                real = acc[pl.ds(at, ks), :rows] - acc[pl.ds(at + kc, ks), rows:]
-                imag = acc[pl.ds(at + kc, ks), :rows] + acc[pl.ds(at, ks), rows:]
-                refs[p][0] = pack(real, imag, odd)
-
-        by_parity(pos_ref, finish)
-    else:
-        new_ref, row_ref, sum_scr = refs[:3]
-        real = acc[:kc, :rows] + acc[kc:, rows:]
-        imag = acc[kc:, :rows] - acc[:kc, rows:]
-        new_ref[0, 0] = real
-        new_ref[0, 1] = imag
-        part = jnp.sum(real * real + imag * imag, axis=0, keepdims=True)
-
-        @pl.when(f == 0)
-        def _():
-            sum_scr[...] = part
-
-        @pl.when(f > 0)
-        def _():
-            sum_scr[...] += part
-
-        @pl.when(f == pl.num_programs(0) - 1)
-        def _():
-            row_ref[...] = lane_fold(sum_scr[...])
+    total = 0.0
+    for f in range(loc):
+        by_parity(pos_ref, lambda odd: load(f, odd))
+        both = r_ref[f].reshape(2 * rows, r_ref.shape[3])
+        acc[...] = lax.dot_general(v_scr[...], both, dims, preferred_element_type=jnp.float32)
+        if not back:
+            by_parity(pos_ref, lambda odd: shares(f, odd))
+        else:
+            real = acc[:kc, :rows] + acc[kc:, rows:]
+            imag = acc[kc:, :rows] - acc[:kc, rows:]
+            refs[0][f, 0] = real
+            refs[0][f, 1] = imag
+            total = total + jnp.sum(real * real + imag * imag, axis=0, keepdims=True)
+    if back:
+        refs[1][...] = lane_fold(total)
 
 
 def product(pos, reflection, blocks, groups, back=False):
     loc, _, rows, cols = reflection.shape
     kc, wide = blocks[0].shape[1:]
     count = len(blocks) // 2
-    whole = lambda *tail: pl.BlockSpec((1,) + tail, lambda f, pos: (f,) + (0,) * len(tail))
-    fixed = lambda *shape: pl.BlockSpec(shape, lambda f, pos: (0,) * len(shape))
-    in_specs = [whole(2, rows, cols)] + [whole(kc, wide)] * (2 * count)
-    operands = [pos, reflection] + list(blocks)
-    scratch = []
     if not back:
-        ks = kc // groups
-        out_shape = [jax.ShapeDtypeStruct((loc, ks, wide), jnp.float32)] * groups
-        out_specs = [whole(ks, wide)] * groups
+        out_shape = [jax.ShapeDtypeStruct((loc, kc // groups, wide), jnp.float32)] * groups
     else:
         out_shape = [
             jax.ShapeDtypeStruct((loc, 2, kc, rows), jnp.float32),
             jax.ShapeDtypeStruct((1, LANES), jnp.float32),
         ]
-        out_specs = [whole(2, kc, rows), fixed(1, LANES)]
-        scratch = [pltpu.VMEM((1, rows), jnp.float32)]
     return pl.pallas_call(
         lambda *refs: product_kernel(groups, count, back, *refs),
-        grid_spec=pltpu.PrefetchScalarGridSpec(
-            num_scalar_prefetch=1,
-            grid=(loc,),
-            in_specs=in_specs,
-            out_specs=out_specs,
-            scratch_shapes=scratch
-            + [
-                pltpu.VMEM((2 * kc, cols), jnp.bfloat16),
-                pltpu.VMEM((2 * kc, 2 * rows), jnp.float32),
-            ],
-        ),
+        in_specs=[SMEM] + [VMEM] * (1 + 2 * count),
+        out_specs=[VMEM] * len(out_shape),
+        scratch_shapes=[
+            pltpu.VMEM((2 * kc, cols), jnp.bfloat16),
+            pltpu.VMEM((2 * kc, 2 * rows), jnp.float32),
+        ],
         out_shape=out_shape,
-        cost_estimate=cost(8 * loc * rows * kc * cols, 2 * reflection.size + 4 * loc * kc * cols),
-        compiler_params=pltpu.CompilerParams(dimension_semantics=("arbitrary",)),
+        cost_estimate=cost(8 * loc * rows * cols * kc, 2 * reflection.size + 4 * loc * kc * cols),
+        compiler_params=GRANT,
         name="product_back" if back else "product",
-    )(*operands)
+    )(pos, reflection, *blocks)
 
 
 def turn_of(limit):
@@ -464,6 +443,7 @@
         out_specs=[VMEM] * len(out_shape),
         scratch_shapes=scratch,
         cost_estimate=cost(40 * size, 8 * size),
+        compiler_params=GRANT,
         name="gate_sum" if squares else "gate_mix" if bases else "gate",
     )(pos, limits, *more, *shares)
 
@@ -491,31 +471,60 @@
         in_specs=[SMEM] + [VMEM] * groups,
         out_specs=VMEM,
         cost_estimate=cost(0, 4 * groups * shares[0].size),
+        compiler_params=GRANT,
         name="join",
     )(pos, *shares)
 
 
-def finish_kernel(groups, pos_ref, t_ref, res_ref, foc_ref, dir_ref, *refs):
-    row_ref, refs = refs[0], refs[1:]
-    image, kept, di, fi = [refs[i * groups : (i + 1) * groups] for i in range(4)]
-    nres_ref, nfoc_ref, green_ref, sent_ref, corr_scr = refs[4 * groups :]
+def update_kernel(groups, pos_ref, t_ref, res_ref, foc_ref, dir_ref, *refs):
+    image = refs[:groups]
+    nres_ref, nfoc_ref = refs[groups:]
     alpha, _ = alpha_of(t_ref)
     me = pos_ref[0]
-    loc, ks, _ = di[0].shape
+    loc, ks, _ = image[0].shape
     nfoc_ref[...] = foc_ref[...] + alpha * dir_ref[...]
 
     def body(odd):
         for p in range(groups):
             rows = pl.ds(pl.multiple_of(share_of(me, p, groups) * ks, ks), ks)
             for f in range(loc):
-                seen = image[p][f]
-                row = (fi[p][f] - kept[p][f]) + alpha * (di[p][f] - seen)
+                for c in range(2):
+                    seen = unpack(image[p][f], c, odd)
+                    nres_ref[f, c, rows, :] = res_ref[f, c, rows, :] - alpha * seen
+
+    by_parity(pos_ref, body)
+
+
+def update(pos, sums, residual, focusing, direction, image, groups):
+    size = residual.size
+    return pl.pallas_call(
+        lambda *refs: update_kernel(groups, *refs),
+        out_shape=[jax.ShapeDtypeStruct(residual.shape, jnp.float32)] * 2,
+        in_specs=[SMEM] + [VMEM] * (4 + groups),
+        out_specs=[VMEM] * 2,
+        cost_estimate=cost(4 * size, 24 * size),
+        compiler_params=GRANT,
+        name="update",
+    )(pos, sums, residual, focusing, direction, *image)
+
+
+def green_kernel(groups, pos_ref, t_ref, nfoc_ref, row_ref, *refs):
+    image, kept, di, fi = [refs[i * groups : (i + 1) * groups] for i in range(4)]
+    green_ref, sent_ref, corr_scr = refs[4 * groups :]
+    alpha, _ = alpha_of(t_ref)
+    me = pos_ref[0]
+    loc, ks, _ = di[0].shape
+
+    def body(odd):
+        for p in range(groups):
+            rows = pl.ds(pl.multiple_of(share_of(me, p, groups) * ks, ks), ks)
+            for f in range(loc):
+                row = (fi[p][f] - kept[p][f]) + alpha * (di[p][f] - image[p][f])
                 for c in range(2):
                     green_ref[f, c, rows, :] = unpack(row, c, odd)
-                    nres_ref[f, c, rows, :] = res_ref[f, c, rows, :] - alpha * unpack(seen, c, odd)
 
     by_parity(pos_ref, body)
-    ones = jnp.ones((8, dir_ref.shape[3]), jnp.float32)
+    ones = jnp.ones((8, nfoc_ref.shape[3]), jnp.float32)
     dims = (((1,), (1,)), ((), ()))
     for f in range(loc):
         gr, gi, fr, fm = green_ref[f, 0], green_ref[f, 1], nfoc_ref[f, 0], nfoc_ref[f, 1]
@@ -528,19 +537,22 @@
     sent_ref[...] = jnp.broadcast_to(table[None], sent_ref.shape)
 
 
-def finish(pos, sums, residual, focusing, direction, row, image, kept, di, fi, groups):
-    loc, _, k, _ = residual.shape
-    size = residual.size
+def green(pos, sums, new_focusing, row, image, kept, di, fi, groups):
+    loc, _, k, _ = new_focusing.shape
+    size = new_focusing.size
     return pl.pallas_call(
-        lambda *refs: finish_kernel(groups, *refs),
-        out_shape=[jax.ShapeDtypeStruct(residual.shape, jnp.float32)] * 3
-        + [jax.ShapeDtypeStruct((sums.shape[0], 4 * loc, LANES), jnp.float32)],
-        in_specs=[SMEM] + [VMEM] * (5 + 4 * groups),
-        out_specs=[VMEM] * 4,
+        lambda *refs: green_kernel(groups, *refs),
+        out_shape=[
+            jax.ShapeDtypeStruct(new_focusing.shape, jnp.float32),
+            jax.ShapeDtypeStruct((sums.shape[0], 4 * loc, LANES), jnp.float32),
+        ],
+        in_specs=[SMEM] + [VMEM] * (3 + 4 * groups),
+        out_specs=[VMEM] * 2,
         scratch_shapes=[pltpu.VMEM((2 * loc, k), jnp.float32)],
-        cost_estimate=cost(14 * size, 40 * size),
-        name="finish",
-    )(pos, sums, residual, focusing, direction, row, *image, *kept, *di, *fi)
+        cost_estimate=cost(12 * size, 24 * size),
+        compiler_params=GRANT,
+        name="green",
+    )(pos, sums, new_focusing, row, *image, *kept, *di, *fi)
 
 
 def turn(pos, sums, new_sums, new_gradient, direction, ranks):
@@ -569,6 +581,7 @@
             jax.ShapeDtypeStruct((loc, 2, points), jnp.float32),
         ],
         cost_estimate=cost(2 * size, 12 * size),
+        compiler_params=GRANT,
         name="turn",
     )(pos, sums, new_sums, new_gradient, direction)
 
@@ -660,10 +673,11 @@
     kept = gate(pos, limits, exchange(fi, groups), groups)
     kept = exchange(kept, groups)
     image = exchange(image_there, groups)
+    new_residual, new_focusing = update(
+        pos, sums, residual, focusing, direction, image, groups
+    )
     new_gradient, row = product(pos, reflection, blocks, groups, True)
-    new_residual, new_focusing, green_field, new_sent = finish(
-        pos, sums, residual, focusing, direction, row, image, kept, di, fi, groups
-    )
+    green_field, new_sent = green(pos, sums, new_focusing, row, image, kept, di, fi, groups)
     new_sums = total_over_all(new_sent)
     new_direction, focal_correlation = turn(pos, sums, new_sums, new_gradient, direction, ranks)
     back = lambda v: jnp.transpose(v, (0, 3, 1, 2))

time: 251 us -> 242 us (0.964)
  Pallas kernels: 61.5 us -> 41.2 us
  local copies, waits for them, and re-layouts: 6.34 us -> 10.9 us
    pallas_call x3, Pallas kernels: 26 us -> 19.5 us  [product(): pl.pallas_call(lambda *refs: product_kernel(groups, count, back, *refs),...]
    pallas_call x4, Pallas kernels: 17.3 us -> 11.3 us  [gate(): pl.pallas_call(lambda *refs: gate_kernel(groups, squares, bool(bases), *r...]
    unnamed x76 -> x54, local copies, waits for them, and re-layouts: 5.73 us -> 10.8 us
    ppermute x18, waiting for transfers between devices: 20.8 us -> 25.1 us  [exchange(): out.append(lax.ppermute(shares[p], 'freq', pairs))]
    pallas_call x2, Pallas kernels: 4.33 us -> 1.29 us  [prep_low(): pl.pallas_call(prep_low_kernel, out_shape=jax.ShapeDtypeStruct((loc, k, 2...]
    pallas_call x1 -> x2, Pallas kernels: 6.07 us -> 4.97 us  [the longest x1 2.54 us: update(): pl.pallas_call(lambda *refs: update_kernel(groups, *refs), out_shape=[jax...]
  transfers between devices with their start and end apart: 46 -> 46, of which waited for: 19 -> 20; matrix products, arithmetic and copies ran while one was open for 1% -> 2% of each run, Pallas kernels for 20% -> 15%
where the time goes in v1:
time: 242 us; the launch traced here: 241 us
  waiting for transfers between devices  104 us (43%)
  starting transfers between devices  68.2 us (28%)
  Pallas kernels  41.2 us (17%)
  blocking collectives  11.9 us (5%)
  local copies, waits for them, and re-layouts  10.9 us (5%)
  other arithmetic  3.7 us (2%)
    ppermute x27, waiting for transfers between devices, move(): return lax.ppermute(v, 'rcv', pairs)  71.6 us
    ppermute x27, starting transfers between devices, move(): return lax.ppermute(v, 'rcv', pairs)  45.7 us
    ppermute x18, waiting for transfers between devices, exchange(): out.append(lax.ppermute(shares[p], 'freq', pairs))  25.1 us
    pallas_call x3, Pallas kernels, product(): pl.pallas_call(lambda *refs: product_kernel(groups, count, back, *refs),...  19.5 us
    ppermute x18, starting transfers between devices, exchange(): out.append(lax.ppermute(shares[p], 'freq', pairs))  12.6 us
    all_to_all x1, blocking collectives, total_over_all(): lax.all_to_all(sent, ('freq', 'rcv'), split_axis=0, concat_axis=0, tiled=...  11.9 us
    pallas_call x4, Pallas kernels, gate(): pl.pallas_call(lambda *refs: gate_kernel(groups, squares, bool(bases), *r...  11.3 us
    unnamed x54, local copies, waits for them, and re-layouts  10.8 us
  transfers between devices with their start and end apart: 46, of which 20 were waited for; matrix products, arithmetic and copies ran while one was open for 2% of the time, Pallas kernels for 15%

profile of v1, /device:TPU:0, one launch (start us, length us, event | category | flops | bytes accessed | tf_op | source)
XLA Modules:
  0.0 241.0 jit_solution(1478775551515600199)
XLA Ops:
  2.7 3.1 %collective-permute-start.5 = (bf16[2,192,640]{2,1,0:T(8,128)(2,1)S(1)}, bf16[2,192,640]{2,1,0:T(8,128)(2,1)}, u32[]{:S(2)}, u32[]{:S(2)}) collective-permute-start(bf16[2,192,640]{2,1,0:T(8,128)(2,1)S(1)} %prep_low.3.refs_2_), channel_id=1, source_target_pairs={{0,2},{1,3},{2,0},{3,1},{4,6},{5,7},{6,4},{7,5},{8,10},{9,11},{10,... | collective-permute-start | bytes 1474568 | tf_op jit(solution)/shard_map/ppermute | solution.py:614
  6.5 10.6 %collective-permute-done.5.refs_4_ = bf16[2,192,640]{2,1,0:T(8,128)(2,1)} collective-permute-done((bf16[2,192,640]{2,1,0:T(8,128)(2,1)S(1)}, bf16[2,192,640]{2,1,0:T(8,128)(2,1)}, u32[]{:S(2)}, u32[]{:S(2)}) %collective-permute-start.5) | collective-permute-done | bytes 491552 | tf_op jit(solution)/shard_map/ppermute | solution.py:614
  17.8 1.3 collective-permute-start.8
  19.1 1.3 collective-permute-start.11
  20.4 1.9 collective-permute-start.4
  23.0 14.5 %collective-permute-start = (bf16[2,192,640]{2,1,0:T(8,128)(2,1)S(1)}, bf16[2,192,640]{2,1,0:T(8,128)(2,1)}, u32[]{:S(2)}, u32[]{:S(2)}) collective-permute-start(bf16[2,192,640]{2,1,0:T(8,128)(2,1)S(1)} %prep_low.2.refs_2_), channel_id=1, source_target_pairs={{0,2},{1,3},{2,0},{3,1},{4,6},{5,7},{6,4},{7,5},{8,10},{9,11},{10,... | collective-permute-start | bytes 1474568 | tf_op jit(solution)/shard_map/ppermute | solution.py:614
  37.5 1.5 collective-permute-start.2
  40.7 5.8 %collective-permute-done.11 = bf16[2,192,640]{2,1,0:T(8,128)(2,1)} collective-permute-done((bf16[2,192,640]{2,1,0:T(8,128)(2,1)S(1)}, bf16[2,192,640]{2,1,0:T(8,128)(2,1)}, u32[]{:S(2)}, u32[]{:S(2)}) %collective-permute-start.11) | collective-permute-done | bytes 491552 | tf_op jit(solution)/shard_map/ppermute | solution.py:614
  46.5 1.6 collective-permute-start.9
  49.8 5.1 %collective-permute-done.refs_4_ = bf16[2,192,640]{2,1,0:T(8,128)(2,1)} collective-permute-done((bf16[2,192,640]{2,1,0:T(8,128)(2,1)S(1)}, bf16[2,192,640]{2,1,0:T(8,128)(2,1)}, u32[]{:S(2)}, u32[]{:S(2)}) %collective-permute-start) | collective-permute-done | bytes 491552 | tf_op jit(solution)/shard_map/ppermute | solution.py:614
  54.9 1.4 collective-permute-start.1
  57.6 6.2 %collective-permute-done.9.refs_7_ = bf16[2,192,640]{2,1,0:T(8,128)(2,1)S(1)} collective-permute-done((bf16[2,192,640]{2,1,0:T(8,128)(2,1)S(1)}, bf16[2,192,640]{2,1,0:T(8,128)(2,1)S(1)}, u32[]{:S(2)}, u32[]{:S(2)}) %collective-permute-start.9) | collective-permute-done | bytes 491552 | tf_op jit(solution)/shard_map/ppermute | solution.py:614
  63.8 7.1 %collective-permute-done.12.refs_9_ = bf16[2,192,640]{2,1,0:T(8,128)(2,1)S(1)} collective-permute-done((bf16[2,192,640]{2,1,0:T(8,128)(2,1)S(1)}, bf16[2,192,640]{2,1,0:T(8,128)(2,1)S(1)}, u32[]{:S(2)}, u32[]{:S(2)}) %collective-permute-start.12) | collective-permute-done | bytes 491552 | tf_op jit(solution)/shard_map/ppermute | solution.py:614
  71.0 2.9 %copy-done = bf16[2,2,320,2560]{3,2,1,0:T(8,128)(2,1)S(1)} copy-done((bf16[2,2,320,2560]{3,2,1,0:T(8,128)(2,1)S(1)}, bf16[2,2,320,2560]{3,2,1,0:T(8,128)(2,1)}, u32[]{:S(2)}) %copy-start) | copy-done | bytes 6553624
  73.8 6.9 %product.2 = (f32[2,48,640]{2,1,0:T(8,128)S(1)}, f32[2,48,640]{2,1,0:T(8,128)S(1)}, f32[2,48,640]{2,1,0:T(8,128)S(1)}, f32[2,48,640]{2,1,0:T(8,128)S(1)}) custom-call(s32[6]{0:T(128)S(1)} %stack.27.pos_ref.refs_0_, bf16[2,2,320,2560]{3,2,1,0:T(8,128)(2,1)S(1)} %copy-done, bf16[2,192,640]{2,1,0:T(8,128)(2,1)S(1)} %prep_low.3.refs_2_, ...), custom_call_target="tpu_custom_call" | custom-call | flops 2516582400 | bytes 10485760 | tf_op jit(solution)/shard_map/product/pallas_call | solution.py:270
  80.8 1.6 collective-permute-start.14
  82.7 1.6 prep_shares.1
  85.4 4.3 %collective-permute-done.14.refs_5_ = f32[2,48,640]{2,1,0:T(8,128)S(1)} collective-permute-done((f32[2,48,640]{2,1,0:T(8,128)S(1)}, f32[2,48,640]{2,1,0:T(8,128)S(1)}, u32[]{:S(2)}, u32[]{:S(2)}) %collective-permute-start.14) | collective-permute-done | bytes 245792 | tf_op jit(solution)/shard_map/ppermute | solution.py:593
  89.7 1.5 collective-permute-start.20
  91.2 2.8 %collective-permute-done.15.refs_6_ = f32[2,48,640]{2,1,0:T(8,128)S(1)} collective-permute-done((f32[2,48,640]{2,1,0:T(8,128)S(1)}, f32[2,48,640]{2,1,0:T(8,128)S(1)}, u32[]{:S(2)}, u32[]{:S(2)}) %collective-permute-start.15) | collective-permute-done | bytes 245792 | tf_op jit(solution)/shard_map/ppermute | solution.py:593
  94.0 1.9 collective-permute-start.21
  95.9 3.1 %gate_sum.1 = (f32[2,48,640]{2,1,0:T(8,128)S(1)}, f32[2,48,640]{2,1,0:T(8,128)S(1)}, f32[2,48,640]{2,1,0:T(8,128)S(1)}, f32[2,48,640]{2,1,0:T(8,128)S(1)}, f32[32,2,128]{2,1,0:T(2,128)}) custom-call(s32[6]{0:T(128)S(1)} %stack.27.pos_ref.refs_0_, s32[192,320]{1,0:T(8,128)S(1)} %bitcast.22, f32[1,128]{1,0:T(1,128)S(1)} %get-tuple-element.46.refs_2_, ...), custom_call_target="tpu_custom_call" | custom-call | flops 9830400 | bytes 1966080 | tf_op jit(solution)/shard_map/gate_sum/pallas_call | solution.py:439
  101.1 10.0 %all-to-all-start = ((f32[32,2,128]{2,1,0:T(2,128)}), f32[32,2,128]{2,1,0:T(2,128)S(1)}, u32[]{:S(2)}, u32[]{:S(2)}) async-start(f32[32,2,128]{2,1,0:T(2,128)} %get-tuple-element.51), calls=%async_computation | async-start | bytes 65536 | tf_op jit(solution)/shard_map/all_to_all | solution.py:639
  111.1 7.2 %all-to-all-done.refs_1_.refs_2_.t_ref = f32[32,2,128]{2,1,0:T(2,128)S(1)} async-done(((f32[32,2,128]{2,1,0:T(2,128)}), f32[32,2,128]{2,1,0:T(2,128)S(1)}, u32[]{:S(2)}, u32[]{:S(2)}) %all-to-all-start) | async-done | bytes 32800 | tf_op jit(solution)/shard_map/all_to_all | solution.py:639
  118.3 1.4 collective-permute-start.37
  120.7 3.0 %gate.2 = (f32[2,48,640]{2,1,0:T(8,128)S(1)}, f32[2,48,640]{2,1,0:T(8,128)S(1)}, f32[2,48,640]{2,1,0:T(8,128)S(1)}, f32[2,48,640]{2,1,0:T(8,128)S(1)}) custom-call(s32[6]{0:T(128)S(1)} %stack.27.pos_ref.refs_0_, s32[192,320]{1,0:T(8,128)S(1)} %bitcast.23, f32[2,48,640]{2,1,0:T(8,128)S(1)} %copy-done.25, f32[2,48,640]{2,1,0:T(8,128)} %collective-permute-done.19.refs_3_, ...), custom_call_target="tpu_custom_call" | custom-call | flops 9830400 | bytes 1966080 | tf_op jit(solution)/shard_map/gate/pallas_call | solution.py:439
  123.7 2.8 %gate_mix.1 = (bf16[2,48,640]{2,1,0:T(8,128)(2,1)S(1)}, bf16[2,48,640]{2,1,0:T(8,128)(2,1)S(1)}, bf16[2,48,640]{2,1,0:T(8,128)(2,1)S(1)}, bf16[2,48,640]{2,1,0:T(8,128)(2,1)S(1)}) custom-call(s32[6]{0:T(128)S(1)} %stack.27.pos_ref.refs_0_, s32[192,320]{1,0:T(8,128)S(1)} %bitcast.24, f32[32,2,128]{2,1,0:T(2,128)S(1)} %all-to-all-done.refs_1_.refs_2_.t_ref, ...), custom_call_target="tpu_custom_call" | custom-call | flops 9830400 | bytes 1966080 | tf_op jit(solution)/shard_map/gate_mix/pallas_call | solution.py:439
  129.2 1.3 collective-permute-start.35
  130.5 2.4 %collective-permute-done.23.refs_3_ = bf16[2,48,640]{2,1,0:T(8,128)(2,1)S(1)} collective-permute-done((bf16[2,48,640]{2,1,0:T(8,128)(2,1)S(1)}, bf16[2,48,640]{2,1,0:T(8,128)(2,1)S(1)}, u32[]{:S(2)}, u32[]{:S(2)}) %collective-permute-start.23) | collective-permute-done | bytes 122912 | tf_op jit(solution)/shard_map/ppermute | solution.py:593
  132.9 1.5 collective-permute-done.24.refs_4_
  135.0 2.8 %collective-permute-start.26 = (bf16[2,192,640]{2,1,0:T(8,128)(2,1)S(1)}, bf16[2,192,640]{2,1,0:T(8,128)(2,1)S(1)}, u32[]{:S(2)}, u32[]{:S(2)}) collective-permute-start(bf16[2,192,640]{2,1,0:T(8,128)(2,1)S(1)} %join.1.refs_2_), channel_id=1, source_target_pairs={{0,2},{1,3},{2,0},{3,1},{4,6},{5,7},{6,4},{7,5},{8,10},{9,11},{10,... | collective-permute-start | bytes 1474568 | tf_op jit(solution)/shard_map/ppermute | solution.py:614
  140.4 2.1 collective-permute-done.34.refs_3_
  143.3 6.5 %collective-permute-done.26.refs_4_ = bf16[2,192,640]{2,1,0:T(8,128)(2,1)S(1)} collective-permute-done((bf16[2,192,640]{2,1,0:T(8,128)(2,1)S(1)}, bf16[2,192,640]{2,1,0:T(8,128)(2,1)S(1)}, u32[]{:S(2)}, u32[]{:S(2)}) %collective-permute-start.26) | collective-permute-done | bytes 491552 | tf_op jit(solution)/shard_map/ppermute | solution.py:614
  153.1 10.5 %collective-permute-done.36.refs_7_ = bf16[2,192,640]{2,1,0:T(8,128)(2,1)S(1)} collective-permute-done((bf16[2,192,640]{2,1,0:T(8,128)(2,1)S(1)}, bf16[2,192,640]{2,1,0:T(8,128)(2,1)S(1)}, u32[]{:S(2)}, u32[]{:S(2)}) %collective-permute-start.36) | collective-permute-done | bytes 491552 | tf_op jit(solution)/shard_map/ppermute | solution.py:614
  164.3 9.3 %collective-permute-done.38.refs_9_ = bf16[2,192,640]{2,1,0:T(8,128)(2,1)S(1)} collective-permute-done((bf16[2,192,640]{2,1,0:T(8,128)(2,1)S(1)}, bf16[2,192,640]{2,1,0:T(8,128)(2,1)S(1)}, u32[]{:S(2)}, u32[]{:S(2)}) %collective-permute-start.38) | collective-permute-done | bytes 491552 | tf_op jit(solution)/shard_map/ppermute | solution.py:614
  175.6 2.9 %copy-done.1 = bf16[2,2,320,2560]{3,2,1,0:T(8,128)(2,1)S(1)} copy-done((bf16[2,2,320,2560]{3,2,1,0:T(8,128)(2,1)S(1)}, bf16[2,2,320,2560]{3,2,1,0:T(8,128)(2,1)}, u32[]{:S(2)}) %copy-start.1) | copy-done | bytes 6553624
  178.5 6.9 %product.3 = (f32[2,48,640]{2,1,0:T(8,128)S(1)}, f32[2,48,640]{2,1,0:T(8,128)S(1)}, f32[2,48,640]{2,1,0:T(8,128)S(1)}, f32[2,48,640]{2,1,0:T(8,128)S(1)}) custom-call(s32[6]{0:T(128)S(1)} %stack.27.pos_ref.refs_0_, bf16[2,2,320,2560]{3,2,1,0:T(8,128)(2,1)S(1)} %copy-done.1, bf16[2,192,640]{2,1,0:T(8,128)(2,1)S(1)} %prep_low.2.refs_2_, ...), custom_call_target="tpu_custom_call" | custom-call | flops 2516582400 | bytes 10485760 | tf_op jit(solution)/shard_map/product/pallas_call | solution.py:270
  185.4 1.8 collective-permute-start.27
  190.3 6.0 %collective-permute-done.40.refs_4_ = f32[2,48,640]{2,1,0:T(8,128)S(1)} collective-permute-done((f32[2,48,640]{2,1,0:T(8,128)S(1)}, f32[2,48,640]{2,1,0:T(8,128)S(1)}, u32[]{:S(2)}, u32[]{:S(2)}) %collective-permute-start.40) | collective-permute-done | bytes 245792 | tf_op jit(solution)/shard_map/ppermute | solution.py:593
  196.5 3.9 %collective-permute-done.41.refs_5_ = f32[2,48,640]{2,1,0:T(8,128)S(1)} collective-permute-done((f32[2,48,640]{2,1,0:T(8,128)S(1)}, f32[2,48,640]{2,1,0:T(8,128)S(1)}, u32[]{:S(2)}, u32[]{:S(2)}) %collective-permute-start.41) | collective-permute-done | bytes 245792 | tf_op jit(solution)/shard_map/ppermute | solution.py:593
  201.3 2.4 gate.3
  203.7 4.2 %collective-permute-done.18.refs_8_.refs_7_ = f32[2,48,640]{2,1,0:T(8,128)S(1)} collective-permute-done((f32[2,48,640]{2,1,0:T(8,128)S(1)}, f32[2,48,640]{2,1,0:T(8,128)S(1)}, u32[]{:S(2)}, u32[]{:S(2)}) %collective-permute-start.18) | collective-permute-done | bytes 245792 | tf_op jit(solution)/shard_map/ppermute | solution.py:593
  210.2 2.5 %update.1 = (f32[2,2,192,320]{3,2,1,0:T(8,128)}, f32[2,2,192,320]{3,2,1,0:T(8,128)}) custom-call(s32[6]{0:T(128)S(1)} %stack.27.pos_ref.refs_0_, f32[32,2,128]{2,1,0:T(2,128)S(1)} %all-to-all-done.refs_1_.refs_2_.t_ref, f32[2,2,192,320]{3,2,1,0:T(8,128)S(1)} %bitcast.19, f32[2,2,192,320]{3,2,1,0:T(8,128)S(1)} %bitcast.21, f32[2,2,192,320]{3,2,1,0:T(8,128)S(1)} %bitcast.16, ...), custom_call_target="tpu_custom_call" | custom-call | flops 983040 | bytes 5898240 | tf_op jit(solution)/shard_map/update/pallas_call | solution.py:500
  212.8 6.2 %collective-permute-done.33.refs_9_ = bf16[2,192,640]{2,1,0:T(8,128)(2,1)S(1)} collective-permute-done((bf16[2,192,640]{2,1,0:T(8,128)(2,1)S(1)}, bf16[2,192,640]{2,1,0:T(8,128)(2,1)S(1)}, u32[]{:S(2)}, u32[]{:S(2)}) %collective-permute-start.33) | collective-permute-done | bytes 491552 | tf_op jit(solution)/shard_map/ppermute | solution.py:614
  219.0 5.7 %product_back.1 = (f32[2,2,192,320]{3,2,1,0:T(8,128)S(1)}, f32[1,128]{1,0:T(1,128)S(1)}) custom-call(s32[6]{0:T(128)S(1)} %stack.27.pos_ref.refs_0_, bf16[2,2,320,2560]{3,2,1,0:T(8,128)(2,1)S(1)} %copy-done.2, bf16[2,192,640]{2,1,0:T(8,128)(2,1)S(1)} %join.1.refs_2_, bf16[2,192,640]{2,1,0:T(8,128)(2,1)S(1)} %collective-permute-done.25.refs_3_, ...), custom_call_target="tpu_custom_call" | custom-call | flops 2516582400 | bytes 10485760 | tf_op jit(solution)/shard_map/product_back/pallas_call | solution.py:270
  224.7 2.4 %green.1 = (f32[2,2,192,320]{3,2,1,0:T(8,128)}, f32[32,8,128]{2,1,0:T(8,128)S(1)}) custom-call(s32[6]{0:T(128)S(1)} %stack.27.pos_ref.refs_0_, f32[32,2,128]{2,1,0:T(2,128)S(1)} %all-to-all-done.refs_1_.refs_2_.t_ref, f32[2,2,192,320]{3,2,1,0:T(8,128)S(1)} %copy-done.9, f32[1,128]{1,0:T(1,128)S(1)} %get-tuple-element.71.refs_3_, ...), custom_call_target="tpu_custom_call" | custom-call | flops 2949120 | bytes 5898240 | tf_op jit(solution)/shard_map/green/pallas_call | solution.py:543
  227.1 11.9 %all_to_all.10.g_ref = f32[32,8,128]{2,1,0:T(8,128)S(1)} all-to-all(f32[32,8,128]{2,1,0:T(8,128)S(1)} %get-tuple-element.82), channel_id=1, replica_groups=mesh['freq'=4,'rcv'=8] {'freq','rcv'}, dimensions={0} | all-to-all | bytes 262144 | tf_op jit(solution)/shard_map/all_to_all | solution.py:639
  239.0 1.9 turn.1
  (120 shorter events, 32.1 us)
Async XLA Ops:
  2.7 14.4 %collective-permute-start.5 = (bf16[2,192,640]{2,1,0:T(8,128)(2,1)S(1)}, bf16[2,192,640]{2,1,0:T(8,128)(2,1)}, u32[]{:S(2)}, u32[]{:S(2)}) collective-permute-start(bf16[2,192,640]{2,1,0:T(8,128)(2,1)S(1)} %prep_low.3.refs_2_), channel_id=1, source_target_pairs={{0,2},{1,3},{2,0},{3,1},{4,6},{5,7},{6,4},{7,5},{8,10},{9,11},{10,... | collective-permute-start | bytes 1474568 | tf_op jit(solution)/shard_map/ppermute | solution.py:614
  5.8 12.0 %collective-permute-start.7 = (bf16[2,192,640]{2,1,0:T(8,128)(2,1)S(1)}, bf16[2,192,640]{2,1,0:T(8,128)(2,1)S(1)}, u32[]{:S(2)}, u32[]{:S(2)}) collective-permute-start(bf16[2,192,640]{2,1,0:T(8,128)(2,1)S(1)} %prep_low.3.refs_2_), channel_id=1, source_target_pairs={{2,4},{3,5},{4,2},{5,3},{10,12},{11,13},{12,10},{13,11},{18,20},{1... | collective-permute-start | bytes 1474568 | tf_op jit(solution)/shard_map/ppermute | solution.py:614
  17.1 2.0 collective-permute-start.10
  17.8 21.2 %collective-permute-start.8 = (bf16[2,192,640]{2,1,0:T(8,128)(2,1)S(1)}, bf16[2,192,640]{2,1,0:T(8,128)(2,1)}, u32[]{:S(2)}, u32[]{:S(2)}) collective-permute-start(bf16[2,192,640]{2,1,0:T(8,128)(2,1)S(1)} %collective-permute-done.7), channel_id=1, source_target_pairs={{2,0},{3,1},{4,6},{5,7},{10,8},{11,9},{12,14},{13,15},{18,16},{19,... | collective-permute-start | bytes 1474568 | tf_op jit(solution)/shard_map/ppermute | solution.py:614
  19.1 27.4 %collective-permute-start.11 = (bf16[2,192,640]{2,1,0:T(8,128)(2,1)S(1)}, bf16[2,192,640]{2,1,0:T(8,128)(2,1)}, u32[]{:S(2)}, u32[]{:S(2)}) collective-permute-start(bf16[2,192,640]{2,1,0:T(8,128)(2,1)S(1)} %collective-permute-done.10), channel_id=1, source_target_pairs={{2,0},{3,1},{4,6},{5,7},{10,8},{11,9},{12,14},{13,15},{18,16},{19,... | collective-permute-start | bytes 1474568 | tf_op jit(solution)/shard_map/ppermute | solution.py:614
  20.4 28.9 %collective-permute-start.4 = (bf16[2,192,640]{2,1,0:T(8,128)(2,1)S(1)}, bf16[2,192,640]{2,1,0:T(8,128)(2,1)}, u32[]{:S(2)}, u32[]{:S(2)}) collective-permute-start(bf16[2,192,640]{2,1,0:T(8,128)(2,1)S(1)} %prep_low.3.refs_2_), channel_id=1, source_target_pairs={{0,1},{1,0},{2,3},{3,2},{4,5},{5,4},{6,7},{7,6},{8,9},{9,8},{10,11... | collective-permute-start | bytes 1474568 | tf_op jit(solution)/shard_map/ppermute | solution.py:614
  23.0 31.9 %collective-permute-start = (bf16[2,192,640]{2,1,0:T(8,128)(2,1)S(1)}, bf16[2,192,640]{2,1,0:T(8,128)(2,1)}, u32[]{:S(2)}, u32[]{:S(2)}) collective-permute-start(bf16[2,192,640]{2,1,0:T(8,128)(2,1)S(1)} %prep_low.2.refs_2_), channel_id=1, source_target_pairs={{0,2},{1,3},{2,0},{3,1},{4,6},{5,7},{6,4},{7,5},{8,10},{9,11},{10,... | collective-permute-start | bytes 1474568 | tf_op jit(solution)/shard_map/ppermute | solution.py:614
  37.5 18.8 %collective-permute-start.2 = (bf16[2,192,640]{2,1,0:T(8,128)(2,1)S(1)}, bf16[2,192,640]{2,1,0:T(8,128)(2,1)}, u32[]{:S(2)}, u32[]{:S(2)}) collective-permute-start(bf16[2,192,640]{2,1,0:T(8,128)(2,1)S(1)} %prep_low.2.refs_2_), channel_id=1, source_target_pairs={{2,4},{3,5},{4,2},{5,3},{10,12},{11,13},{12,10},{13,11},{18,20},{1... | collective-permute-start | bytes 1474568 | tf_op jit(solution)/shard_map/ppermute | solution.py:614
  39.0 18.6 %collective-permute-start.6 = (bf16[2,192,640]{2,1,0:T(8,128)(2,1)}, bf16[2,192,640]{2,1,0:T(8,128)(2,1)S(1)}, u32[]{:S(2)}, u32[]{:S(2)}) collective-permute-start(bf16[2,192,640]{2,1,0:T(8,128)(2,1)} %collective-permute-done.5.refs_4_), channel_id=1, source_target_pairs={{0,1},{1,0},{2,3},{3,2},{4,5},{5,4},{6,7},{7,6},{8,9},{9,8},{10,11... | collective-permute-start | bytes 1474568 | tf_op jit(solution)/shard_map/ppermute | solution.py:614
  39.5 43.2 %copy-start.8 = (f32[2,320,2,192]{1,3,2,0:T(8,128)S(1)}, f32[2,320,2,192]{1,3,2,0:T(8,128)}, u32[]{:S(2)}) copy-start(f32[2,320,2,192]{1,3,2,0:T(8,128)} %param.11) | copy-start | bytes 2949124
  46.5 17.3 %collective-permute-start.9 = (bf16[2,192,640]{2,1,0:T(8,128)(2,1)S(1)}, bf16[2,192,640]{2,1,0:T(8,128)(2,1)S(1)}, u32[]{:S(2)}, u32[]{:S(2)}) collective-permute-start(bf16[2,192,640]{2,1,0:T(8,128)(2,1)S(1)} %broadcast_select_fusion.5.refs_6_), channel_id=1, source_target_pairs={{0,1},{1,0},{2,3},{3,2},{4,5},{5,4},{6,7},{7,6},{8,9},{9,8},{10,11... | collective-permute-start | bytes 1474568 | tf_op jit(solution)/shard_map/ppermute | solution.py:614
  48.1 34.5 %copy-start.5 = (f32[2,320,2,192]{1,3,2,0:T(8,128)S(1)}, f32[2,320,2,192]{1,3,2,0:T(8,128)}, u32[]{:S(2)}) copy-start(f32[2,320,2,192]{1,3,2,0:T(8,128)} %param.9) | copy-start | bytes 2949124
  49.3 21.6 %collective-permute-start.12 = (bf16[2,192,640]{2,1,0:T(8,128)(2,1)S(1)}, bf16[2,192,640]{2,1,0:T(8,128)(2,1)S(1)}, u32[]{:S(2)}, u32[]{:S(2)}) collective-permute-start(bf16[2,192,640]{2,1,0:T(8,128)(2,1)S(1)} %broadcast_select_fusion.4.refs_8_), channel_id=1, source_target_pairs={{0,1},{1,0},{2,3},{3,2},{4,5},{5,4},{6,7},{7,6},{8,9},{9,8},{10,11... | collective-permute-start | bytes 1474568 | tf_op jit(solution)/shard_map/ppermute | solution.py:614
  54.9 56.2 %collective-permute-start.1 = (bf16[2,192,640]{2,1,0:T(8,128)(2,1)}, bf16[2,192,640]{2,1,0:T(8,128)(2,1)}, u32[]{:S(2)}, u32[]{:S(2)}) collective-permute-start(bf16[2,192,640]{2,1,0:T(8,128)(2,1)} %collective-permute-done.refs_4_), channel_id=1, source_target_pairs={{2,4},{3,5},{4,2},{5,3},{10,12},{11,13},{12,10},{13,11},{18,20},{1... | collective-permute-start | bytes 1474568 | tf_op jit(solution)/shard_map/ppermute | solution.py:614
  56.3 54.8 %collective-permute-start.3 = (bf16[2,192,640]{2,1,0:T(8,128)(2,1)}, bf16[2,192,640]{2,1,0:T(8,128)(2,1)}, u32[]{:S(2)}, u32[]{:S(2)}) collective-permute-start(bf16[2,192,640]{2,1,0:T(8,128)(2,1)} %collective-permute-done.2), channel_id=1, source_target_pairs={{2,0},{3,1},{4,6},{5,7},{10,8},{11,9},{12,14},{13,15},{18,16},{19,... | collective-permute-start | bytes 1474568 | tf_op jit(solution)/shard_map/ppermute | solution.py:614
  80.8 4.3 %collective-permute-start.13 = (f32[2,48,640]{2,1,0:T(8,128)S(1)}, f32[2,48,640]{2,1,0:T(8,128)S(1)}, u32[]{:S(2)}, u32[]{:S(2)}) collective-permute-start(f32[2,48,640]{2,1,0:T(8,128)S(1)} %get-tuple-element.48.refs_13_), channel_id=1, source_target_pairs={{0,8},{8,0},{16,24},{24,16},{1,9},{9,1},{17,25},{25,17},{2,10},{10... | collective-permute-start | bytes 737288 | tf_op jit(solution)/shard_map/ppermute | solution.py:593
  80.8 8.9 %collective-permute-start.14 = (f32[2,48,640]{2,1,0:T(8,128)S(1)}, f32[2,48,640]{2,1,0:T(8,128)S(1)}, u32[]{:S(2)}, u32[]{:S(2)}) collective-permute-start(f32[2,48,640]{2,1,0:T(8,128)S(1)} %get-tuple-element.49.refs_14_), channel_id=1, source_target_pairs={{0,16},{8,24},{16,0},{24,8},{1,17},{9,25},{17,1},{25,9},{2,18},{10... | collective-permute-start | bytes 737288 | tf_op jit(solution)/shard_map/ppermute | solution.py:593
  82.4 11.6 %collective-permute-start.15 = (f32[2,48,640]{2,1,0:T(8,128)S(1)}, f32[2,48,640]{2,1,0:T(8,128)S(1)}, u32[]{:S(2)}, u32[]{:S(2)}) collective-permute-start(f32[2,48,640]{2,1,0:T(8,128)S(1)} %get-tuple-element.50.refs_15_), channel_id=1, source_target_pairs={{0,24},{8,16},{16,8},{24,0},{1,25},{9,17},{17,9},{25,1},{2,26},{10... | collective-permute-start | bytes 737288 | tf_op jit(solution)/shard_map/ppermute | solution.py:593
  85.0 34.7 %collective-permute-start.19 = (f32[2,48,640]{2,1,0:T(8,128)}, f32[2,48,640]{2,1,0:T(8,128)}, u32[]{:S(2)}, u32[]{:S(2)}) collective-permute-start(f32[2,48,640]{2,1,0:T(8,128)} %get-tuple-element.60), channel_id=1, source_target_pairs={{0,8},{8,0},{16,24},{24,16},{1,9},{9,1},{17,25},{25,17},{2,10},{10... | collective-permute-start | bytes 737288 | tf_op jit(solution)/shard_map/ppermute | solution.py:593
  89.7 30.0 %collective-permute-start.20 = (f32[2,48,640]{2,1,0:T(8,128)}, f32[2,48,640]{2,1,0:T(8,128)}, u32[]{:S(2)}, u32[]{:S(2)}) collective-permute-start(f32[2,48,640]{2,1,0:T(8,128)} %get-tuple-element.61), channel_id=1, source_target_pairs={{0,16},{8,24},{16,0},{24,8},{1,17},{9,25},{17,1},{25,9},{2,18},{10... | collective-permute-start | bytes 737288 | tf_op jit(solution)/shard_map/ppermute | solution.py:593
  94.0 25.7 %collective-permute-start.21 = (f32[2,48,640]{2,1,0:T(8,128)}, f32[2,48,640]{2,1,0:T(8,128)}, u32[]{:S(2)}, u32[]{:S(2)}) collective-permute-start(f32[2,48,640]{2,1,0:T(8,128)} %get-tuple-element.62), channel_id=1, source_target_pairs={{0,24},{8,16},{16,8},{24,0},{1,25},{9,17},{17,9},{25,1},{2,26},{10... | collective-permute-start | bytes 737288 | tf_op jit(solution)/shard_map/ppermute | solution.py:593
  101.1 17.2 %all-to-all-start = ((f32[32,2,128]{2,1,0:T(2,128)}), f32[32,2,128]{2,1,0:T(2,128)S(1)}, u32[]{:S(2)}, u32[]{:S(2)}) async-start(f32[32,2,128]{2,1,0:T(2,128)} %get-tuple-element.51), calls=%async_computation | async-start | bytes 65536 | tf_op jit(solution)/shard_map/all_to_all | solution.py:639
  118.3 21.4 %collective-permute-start.37 = (bf16[2,192,640]{2,1,0:T(8,128)(2,1)}, bf16[2,192,640]{2,1,0:T(8,128)(2,1)S(1)}, u32[]{:S(2)}, u32[]{:S(2)}) collective-permute-start(bf16[2,192,640]{2,1,0:T(8,128)(2,1)} %collective-permute-done.1), channel_id=1, source_target_pairs={{2,0},{3,1},{4,6},{5,7},{10,8},{11,9},{12,14},{13,15},{18,16},{19,... | collective-permute-start | bytes 1474568 | tf_op jit(solution)/shard_map/ppermute | solution.py:614
  126.6 2.6 %collective-permute-start.22 = (bf16[2,48,640]{2,1,0:T(8,128)(2,1)S(1)}, bf16[2,48,640]{2,1,0:T(8,128)(2,1)S(1)}, u32[]{:S(2)}, u32[]{:S(2)}) collective-permute-start(bf16[2,48,640]{2,1,0:T(8,128)(2,1)S(1)} %get-tuple-element.68), channel_id=1, source_target_pairs={{0,8},{8,0},{16,24},{24,16},{1,9},{9,1},{17,25},{25,17},{2,10},{10... | collective-permute-start | bytes 368648 | tf_op jit(solution)/shard_map/ppermute | solution.py:593
  126.7 6.2 %collective-permute-start.23 = (bf16[2,48,640]{2,1,0:T(8,128)(2,1)S(1)}, bf16[2,48,640]{2,1,0:T(8,128)(2,1)S(1)}, u32[]{:S(2)}, u32[]{:S(2)}) collective-permute-start(bf16[2,48,640]{2,1,0:T(8,128)(2,1)S(1)} %get-tuple-element.69), channel_id=1, source_target_pairs={{0,16},{8,24},{16,0},{24,8},{1,17},{9,25},{17,1},{25,9},{2,18},{10... | collective-permute-start | bytes 368648 | tf_op jit(solution)/shard_map/ppermute | solution.py:593
  127.3 7.1 %collective-permute-start.24 = (bf16[2,48,640]{2,1,0:T(8,128)(2,1)S(1)}, bf16[2,48,640]{2,1,0:T(8,128)(2,1)S(1)}, u32[]{:S(2)}, u32[]{:S(2)}) collective-permute-start(bf16[2,48,640]{2,1,0:T(8,128)(2,1)S(1)} %get-tuple-element.70), channel_id=1, source_target_pairs={{0,24},{8,16},{16,8},{24,0},{1,25},{9,17},{17,9},{25,1},{2,26},{10... | collective-permute-start | bytes 368648 | tf_op jit(solution)/shard_map/ppermute | solution.py:593
  128.5 14.1 %collective-permute-start.34 = (bf16[2,192,640]{2,1,0:T(8,128)(2,1)S(1)}, bf16[2,192,640]{2,1,0:T(8,128)(2,1)S(1)}, u32[]{:S(2)}, u32[]{:S(2)}) collective-permute-start(bf16[2,192,640]{2,1,0:T(8,128)(2,1)S(1)} %prep_low.2.refs_2_), channel_id=1, source_target_pairs={{0,1},{1,0},{2,3},{3,2},{4,5},{5,4},{6,7},{7,6},{8,9},{9,8},{10,11... | collective-permute-start | bytes 1474568 | tf_op jit(solution)/shard_map/ppermute | solution.py:614
  129.2 23.9 %collective-permute-start.35 = (bf16[2,192,640]{2,1,0:T(8,128)(2,1)}, bf16[2,192,640]{2,1,0:T(8,128)(2,1)S(1)}, u32[]{:S(2)}, u32[]{:S(2)}) collective-permute-start(bf16[2,192,640]{2,1,0:T(8,128)(2,1)} %collective-permute-done.refs_4_), channel_id=1, source_target_pairs={{0,1},{1,0},{2,3},{3,2},{4,5},{5,4},{6,7},{7,6},{8,9},{9,8},{10,11... | collective-permute-start | bytes 1474568 | tf_op jit(solution)/shard_map/ppermute | solution.py:614
  135.0 14.8 %collective-permute-start.26 = (bf16[2,192,640]{2,1,0:T(8,128)(2,1)S(1)}, bf16[2,192,640]{2,1,0:T(8,128)(2,1)S(1)}, u32[]{:S(2)}, u32[]{:S(2)}) collective-permute-start(bf16[2,192,640]{2,1,0:T(8,128)(2,1)S(1)} %join.1.refs_2_), channel_id=1, source_target_pairs={{0,2},{1,3},{2,0},{3,1},{4,6},{5,7},{6,4},{7,5},{8,10},{9,11},{10,... | collective-permute-start | bytes 1474568 | tf_op jit(solution)/shard_map/ppermute | solution.py:614
  138.9 24.8 %collective-permute-start.36 = (bf16[2,192,640]{2,1,0:T(8,128)(2,1)S(1)}, bf16[2,192,640]{2,1,0:T(8,128)(2,1)S(1)}, u32[]{:S(2)}, u32[]{:S(2)}) collective-permute-start(bf16[2,192,640]{2,1,0:T(8,128)(2,1)S(1)} %broadcast_select_fusion.1.refs_6_), channel_id=1, source_target_pairs={{0,1},{1,0},{2,3},{3,2},{4,5},{5,4},{6,7},{7,6},{8,9},{9,8},{10,11... | collective-permute-start | bytes 1474568 | tf_op jit(solution)/shard_map/ppermute | solution.py:614
  139.6 10.9 %collective-permute-start.28 = (bf16[2,192,640]{2,1,0:T(8,128)(2,1)S(1)}, bf16[2,192,640]{2,1,0:T(8,128)(2,1)S(1)}, u32[]{:S(2)}, u32[]{:S(2)}) collective-permute-start(bf16[2,192,640]{2,1,0:T(8,128)(2,1)S(1)} %join.1.refs_2_), channel_id=1, source_target_pairs={{2,4},{3,5},{4,2},{5,3},{10,12},{11,13},{12,10},{13,11},{18,20},{1... | collective-permute-start | bytes 1474568 | tf_op jit(solution)/shard_map/ppermute | solution.py:614
  142.6 31.0 %collective-permute-start.38 = (bf16[2,192,640]{2,1,0:T(8,128)(2,1)S(1)}, bf16[2,192,640]{2,1,0:T(8,128)(2,1)S(1)}, u32[]{:S(2)}, u32[]{:S(2)}) collective-permute-start(bf16[2,192,640]{2,1,0:T(8,128)(2,1)S(1)} %broadcast_select_fusion.refs_8_), channel_id=1, source_target_pairs={{0,1},{1,0},{2,3},{3,2},{4,5},{5,4},{6,7},{7,6},{8,9},{9,8},{10,11... | collective-permute-start | bytes 1474568 | tf_op jit(solution)/shard_map/ppermute | solution.py:614
  149.8 24.5 %collective-permute-start.31 = (bf16[2,192,640]{2,1,0:T(8,128)(2,1)S(1)}, bf16[2,192,640]{2,1,0:T(8,128)(2,1)S(1)}, u32[]{:S(2)}, u32[]{:S(2)}) collective-permute-start(bf16[2,192,640]{2,1,0:T(8,128)(2,1)S(1)} %collective-permute-done.26.refs_4_), channel_id=1, source_target_pairs={{2,4},{3,5},{4,2},{5,3},{10,12},{11,13},{12,10},{13,11},{18,20},{1... | collective-permute-start | bytes 1474568 | tf_op jit(solution)/shard_map/ppermute | solution.py:614
  150.5 34.9 %collective-permute-start.29 = (bf16[2,192,640]{2,1,0:T(8,128)(2,1)S(1)}, bf16[2,192,640]{2,1,0:T(8,128)(2,1)S(1)}, u32[]{:S(2)}, u32[]{:S(2)}) collective-permute-start(bf16[2,192,640]{2,1,0:T(8,128)(2,1)S(1)} %collective-permute-done.28), channel_id=1, source_target_pairs={{2,0},{3,1},{4,6},{5,7},{10,8},{11,9},{12,14},{13,15},{18,16},{19,... | collective-permute-start | bytes 1474568 | tf_op jit(solution)/shard_map/ppermute | solution.py:614
  153.1 34.2 %collective-permute-start.16 = (f32[2,48,640]{2,1,0:T(8,128)S(1)}, f32[2,48,640]{2,1,0:T(8,128)S(1)}, u32[]{:S(2)}, u32[]{:S(2)}) collective-permute-start(f32[2,48,640]{2,1,0:T(8,128)S(1)} %copy-done.23), channel_id=1, source_target_pairs={{0,8},{8,0},{16,24},{24,16},{1,9},{9,1},{17,25},{25,17},{2,10},{10... | collective-permute-start | bytes 737288 | tf_op jit(solution)/shard_map/ppermute | solution.py:593
  163.6 23.7 %collective-permute-start.17 = (f32[2,48,640]{2,1,0:T(8,128)S(1)}, f32[2,48,640]{2,1,0:T(8,128)S(1)}, u32[]{:S(2)}, u32[]{:S(2)}) collective-permute-start(f32[2,48,640]{2,1,0:T(8,128)S(1)} %copy-done.21), channel_id=1, source_target_pairs={{0,16},{8,24},{16,0},{24,8},{1,17},{9,25},{17,1},{25,9},{2,18},{10... | collective-permute-start | bytes 737288 | tf_op jit(solution)/shard_map/ppermute | solution.py:593
  173.6 35.2 %collective-permute-start.25 = (bf16[2,192,640]{2,1,0:T(8,128)(2,1)S(1)}, bf16[2,192,640]{2,1,0:T(8,128)(2,1)S(1)}, u32[]{:S(2)}, u32[]{:S(2)}) collective-permute-start(bf16[2,192,640]{2,1,0:T(8,128)(2,1)S(1)} %join.1.refs_2_), channel_id=1, source_target_pairs={{0,1},{1,0},{2,3},{3,2},{4,5},{5,4},{6,7},{7,6},{8,9},{9,8},{10,11... | collective-permute-start | bytes 1474568 | tf_op jit(solution)/shard_map/ppermute | solution.py:614
  174.3 14.5 %collective-permute-start.32 = (bf16[2,192,640]{2,1,0:T(8,128)(2,1)S(1)}, bf16[2,192,640]{2,1,0:T(8,128)(2,1)S(1)}, u32[]{:S(2)}, u32[]{:S(2)}) collective-permute-start(bf16[2,192,640]{2,1,0:T(8,128)(2,1)S(1)} %collective-permute-done.31), channel_id=1, source_target_pairs={{2,0},{3,1},{4,6},{5,7},{10,8},{11,9},{12,14},{13,15},{18,16},{19,... | collective-permute-start | bytes 1474568 | tf_op jit(solution)/shard_map/ppermute | solution.py:614
  185.4 24.0 %collective-permute-start.27 = (bf16[2,192,640]{2,1,0:T(8,128)(2,1)S(1)}, bf16[2,192,640]{2,1,0:T(8,128)(2,1)S(1)}, u32[]{:S(2)}, u32[]{:S(2)}) collective-permute-start(bf16[2,192,640]{2,1,0:T(8,128)(2,1)S(1)} %collective-permute-done.26.refs_4_), channel_id=1, source_target_pairs={{0,1},{1,0},{2,3},{3,2},{4,5},{5,4},{6,7},{7,6},{8,9},{9,8},{10,11... | collective-permute-start | bytes 1474568 | tf_op jit(solution)/shard_map/ppermute | solution.py:614
  187.3 2.0 collective-permute-start.39
  187.4 8.9 %collective-permute-start.40 = (f32[2,48,640]{2,1,0:T(8,128)S(1)}, f32[2,48,640]{2,1,0:T(8,128)S(1)}, u32[]{:S(2)}, u32[]{:S(2)}) collective-permute-start(f32[2,48,640]{2,1,0:T(8,128)S(1)} %get-tuple-element.76.refs_18_), channel_id=1, source_target_pairs={{0,16},{8,24},{16,0},{24,8},{1,17},{9,25},{17,1},{25,9},{2,18},{10... | collective-permute-start | bytes 737288 | tf_op jit(solution)/shard_map/ppermute | solution.py:593
  188.8 11.6 %collective-permute-start.41 = (f32[2,48,640]{2,1,0:T(8,128)S(1)}, f32[2,48,640]{2,1,0:T(8,128)S(1)}, u32[]{:S(2)}, u32[]{:S(2)}) collective-permute-start(f32[2,48,640]{2,1,0:T(8,128)S(1)} %get-tuple-element.77.refs_19_), channel_id=1, source_target_pairs={{0,24},{8,16},{16,8},{24,0},{1,25},{9,17},{17,9},{25,1},{2,26},{10... | collective-permute-start | bytes 737288 | tf_op jit(solution)/shard_map/ppermute | solution.py:593
  189.3 23.4 %collective-permute-start.30 = (bf16[2,192,640]{2,1,0:T(8,128)(2,1)S(1)}, bf16[2,192,640]{2,1,0:T(8,128)(2,1)S(1)}, u32[]{:S(2)}, u32[]{:S(2)}) collective-permute-start(bf16[2,192,640]{2,1,0:T(8,128)(2,1)S(1)} %broadcast_select_fusion.3.refs_6_), channel_id=1, source_target_pairs={{0,1},{1,0},{2,3},{3,2},{4,5},{5,4},{6,7},{7,6},{8,9},{9,8},{10,11... | collective-permute-start | bytes 1474568 | tf_op jit(solution)/shard_map/ppermute | solution.py:614
  196.3 22.7 %collective-permute-start.33 = (bf16[2,192,640]{2,1,0:T(8,128)(2,1)S(1)}, bf16[2,192,640]{2,1,0:T(8,128)(2,1)S(1)}, u32[]{:S(2)}, u32[]{:S(2)}) collective-permute-start(bf16[2,192,640]{2,1,0:T(8,128)(2,1)S(1)} %broadcast_select_fusion.2.refs_8_), channel_id=1, source_target_pairs={{0,1},{1,0},{2,3},{3,2},{4,5},{5,4},{6,7},{7,6},{8,9},{9,8},{10,11... | collective-permute-start | bytes 1474568 | tf_op jit(solution)/shard_map/ppermute | solution.py:614
  200.5 7.4 %collective-permute-start.18 = (f32[2,48,640]{2,1,0:T(8,128)S(1)}, f32[2,48,640]{2,1,0:T(8,128)S(1)}, u32[]{:S(2)}, u32[]{:S(2)}) collective-permute-start(f32[2,48,640]{2,1,0:T(8,128)S(1)} %copy-done.19), channel_id=1, source_target_pairs={{0,24},{8,16},{16,8},{24,0},{1,25},{9,17},{17,9},{25,1},{2,26},{10... | collective-permute-start | bytes 737288 | tf_op jit(solution)/shard_map/ppermute | solution.py:593
  207.9 16.8 %collective-permute-start.42 = (f32[2,48,640]{2,1,0:T(8,128)S(1)}, f32[2,48,640]{2,1,0:T(8,128)S(1)}, u32[]{:S(2)}, u32[]{:S(2)}) collective-permute-start(f32[2,48,640]{2,1,0:T(8,128)S(1)} %get-tuple-element.79), channel_id=1, source_target_pairs={{0,8},{8,0},{16,24},{24,16},{1,9},{9,1},{17,25},{25,17},{2,10},{10... | collective-permute-start | bytes 737288 | tf_op jit(solution)/shard_map/ppermute | solution.py:593
  208.8 15.8 %collective-permute-start.43 = (f32[2,48,640]{2,1,0:T(8,128)S(1)}, f32[2,48,640]{2,1,0:T(8,128)S(1)}, u32[]{:S(2)}, u32[]{:S(2)}) collective-permute-start(f32[2,48,640]{2,1,0:T(8,128)S(1)} %get-tuple-element.80), channel_id=1, source_target_pairs={{0,16},{8,24},{16,0},{24,8},{1,17},{9,25},{17,1},{25,9},{2,18},{10... | collective-permute-start | bytes 737288 | tf_op jit(solution)/shard_map/ppermute | solution.py:593
  209.5 15.2 %collective-permute-start.44 = (f32[2,48,640]{2,1,0:T(8,128)S(1)}, f32[2,48,640]{2,1,0:T(8,128)S(1)}, u32[]{:S(2)}, u32[]{:S(2)}) collective-permute-start(f32[2,48,640]{2,1,0:T(8,128)S(1)} %get-tuple-element.81), channel_id=1, source_target_pairs={{0,24},{8,16},{16,8},{24,0},{1,25},{9,17},{17,9},{25,1},{2,26},{10... | collective-permute-start | bytes 737288 | tf_op jit(solution)/shard_map/ppermute | solution.py:593
  (25 other events, 220.4 us)

commit v2 on v1

--- a/solution.py
+++ b/solution.py
@@ -344,7 +344,8 @@
     return outs
 
 
-def gate_kernel(groups, squares, mixed, pos_ref, s_ref, *refs):
+def gate_kernel(groups, squares, mixed, near, pos_ref, s_ref, *refs):
+    refs = refs[near:]
     if squares:
         row_ref, refs = refs[0], refs[1:]
     if mixed:
@@ -417,7 +418,7 @@
         sum_ref[...] = jnp.broadcast_to(both[None], sum_ref.shape)
 
 
-def gate(pos, limits, shares, groups, row=None, devices=0, sums=None, bases=()):
+def gate(pos, limits, shares, groups, row=None, devices=0, sums=None, bases=(), near=None):
     squares = row is not None
     loc, ks, wide = shares[0].shape
     kind = jnp.bfloat16 if bases else jnp.float32
@@ -430,6 +431,8 @@
         more = [row]
     if bases:
         more = [sums, *bases]
+    if near is not None:
+        more = [near]
     scratch = scratch + [
         pltpu.VMEM((groups * loc, ks, wide), jnp.float32),
         pltpu.VMEM((groups * loc, ks, wide), jnp.float32),
@@ -437,7 +440,7 @@
     ]
     size = groups * loc * ks * wide
     return pl.pallas_call(
-        lambda *refs: gate_kernel(groups, squares, bool(bases), *refs),
+        lambda *refs: gate_kernel(groups, squares, bool(bases), near is not None, *refs),
         out_shape=out_shape,
         in_specs=[SMEM, VMEM] + [VMEM] * (groups + len(more)),
         out_specs=[VMEM] * len(out_shape),
@@ -656,7 +659,7 @@
     blocks = spread_all(prep_low(pos, direction), mid)
     *res_shares, gamma_row = prep_shares(pos, residual, gradient, groups)
     res_there = exchange(res_shares, groups)
-    kept_res = gate(pos, limits, res_there, groups)
+    kept_res = gate(pos, limits, res_there, groups, near=reflection)
     foc_own = prep_low(pos, focusing)
     aside = spread(foc_own, mid)
     next(aside)

time: 242 us -> 243 us (level)
    ppermute x27, waiting for transfers between devices: 71.6 us -> 75.7 us  [move(): return lax.ppermute(v, 'rcv', pairs)]
    ppermute x18, waiting for transfers between devices: 25.1 us -> 22.6 us  [exchange(): out.append(lax.ppermute(shares[p], 'freq', pairs))]
where the time goes in v2:
time: 243 us; the launch traced here: 242 us
  waiting for transfers between devices  105 us (43%)
  starting transfers between devices  67.3 us (28%)
  Pallas kernels  42.3 us (17%)
  local copies, waits for them, and re-layouts  11.7 us (5%)
  blocking collectives  10.8 us (4%)
  other arithmetic  3.71 us (2%)
    ppermute x27, waiting for transfers between devices, move(): return lax.ppermute(v, 'rcv', pairs)  75.7 us
    ppermute x27, starting transfers between devices, move(): return lax.ppermute(v, 'rcv', pairs)  44.9 us
    ppermute x18, waiting for transfers between devices, exchange(): out.append(lax.ppermute(shares[p], 'freq', pairs))  22.6 us
    pallas_call x3, Pallas kernels, product(): pl.pallas_call(lambda *refs: product_kernel(groups, count, back, *refs),...  19.6 us
    ppermute x18, starting transfers between devices, exchange(): out.append(lax.ppermute(shares[p], 'freq', pairs))  12.1 us
    unnamed x54, local copies, waits for them, and re-layouts  11.6 us
    pallas_call x4, Pallas kernels, gate(): pl.pallas_call(lambda *refs: gate_kernel(groups, squares, bool(bases), ne...  11.4 us
    all_to_all x1, blocking collectives, total_over_all(): lax.all_to_all(sent, ('freq', 'rcv'), split_axis=0, concat_axis=0, tiled=...  10.8 us
  transfers between devices with their start and end apart: 46, of which 20 were waited for; matrix products, arithmetic and copies ran while one was open for 2% of the time, Pallas kernels for 15%

profile of v2, /device:TPU:0, one launch (start us, length us, event | category | flops | bytes accessed | tf_op | source)
XLA Modules:
  0.0 242.3 jit_solution(14319552159965700390)
XLA Ops:
  2.0 1.4 prep_low.3.refs_2_
  3.4 3.1 %collective-permute-start.5 = (bf16[2,192,640]{2,1,0:T(8,128)(2,1)}, bf16[2,192,640]{2,1,0:T(8,128)(2,1)}, u32[]{:S(2)}, u32[]{:S(2)}) collective-permute-start(bf16[2,192,640]{2,1,0:T(8,128)(2,1)} %prep_low.3.refs_2_), channel_id=1, source_target_pairs={{0,2},{1,3},{2,0},{3,1},{4,6},{5,7},{6,4},{7,5},{8,10},{9,11},{10,... | collective-permute-start | bytes 1474568 | tf_op jit(solution)/shard_map/ppermute | solution.py:617
  7.2 10.8 %collective-permute-done.5.refs_4_ = bf16[2,192,640]{2,1,0:T(8,128)(2,1)} collective-permute-done((bf16[2,192,640]{2,1,0:T(8,128)(2,1)}, bf16[2,192,640]{2,1,0:T(8,128)(2,1)}, u32[]{:S(2)}, u32[]{:S(2)}) %collective-permute-start.5) | collective-permute-done | bytes 491552 | tf_op jit(solution)/shard_map/ppermute | solution.py:617
  21.3 1.9 collective-permute-start.4
  23.9 13.8 %collective-permute-start = (bf16[2,192,640]{2,1,0:T(8,128)(2,1)S(1)}, bf16[2,192,640]{2,1,0:T(8,128)(2,1)}, u32[]{:S(2)}, u32[]{:S(2)}) collective-permute-start(bf16[2,192,640]{2,1,0:T(8,128)(2,1)S(1)} %prep_low.2.refs_2_), channel_id=1, source_target_pairs={{0,2},{1,3},{2,0},{3,1},{4,6},{5,7},{6,4},{7,5},{8,10},{9,11},{10,... | collective-permute-start | bytes 1474568 | tf_op jit(solution)/shard_map/ppermute | solution.py:617
  37.7 1.5 collective-permute-start.2
  40.9 6.4 %collective-permute-done.11 = bf16[2,192,640]{2,1,0:T(8,128)(2,1)S(1)} collective-permute-done((bf16[2,192,640]{2,1,0:T(8,128)(2,1)S(1)}, bf16[2,192,640]{2,1,0:T(8,128)(2,1)S(1)}, u32[]{:S(2)}, u32[]{:S(2)}) %collective-permute-start.11) | collective-permute-done | bytes 491552 | tf_op jit(solution)/shard_map/ppermute | solution.py:617
  48.1 1.6 collective-permute-start.9
  51.4 4.4 %collective-permute-done.refs_4_ = bf16[2,192,640]{2,1,0:T(8,128)(2,1)} collective-permute-done((bf16[2,192,640]{2,1,0:T(8,128)(2,1)S(1)}, bf16[2,192,640]{2,1,0:T(8,128)(2,1)}, u32[]{:S(2)}, u32[]{:S(2)}) %collective-permute-start) | collective-permute-done | bytes 491552 | tf_op jit(solution)/shard_map/ppermute | solution.py:617
  55.8 1.4 collective-permute-start.1
  58.5 5.5 %collective-permute-done.9.refs_7_ = bf16[2,192,640]{2,1,0:T(8,128)(2,1)S(1)} collective-permute-done((bf16[2,192,640]{2,1,0:T(8,128)(2,1)S(1)}, bf16[2,192,640]{2,1,0:T(8,128)(2,1)S(1)}, u32[]{:S(2)}, u32[]{:S(2)}) %collective-permute-start.9) | collective-permute-done | bytes 491552 | tf_op jit(solution)/shard_map/ppermute | solution.py:617
  64.0 7.1 %collective-permute-done.12.refs_9_ = bf16[2,192,640]{2,1,0:T(8,128)(2,1)S(1)} collective-permute-done((bf16[2,192,640]{2,1,0:T(8,128)(2,1)S(1)}, bf16[2,192,640]{2,1,0:T(8,128)(2,1)S(1)}, u32[]{:S(2)}, u32[]{:S(2)}) %collective-permute-start.12) | collective-permute-done | bytes 491552 | tf_op jit(solution)/shard_map/ppermute | solution.py:617
  71.2 2.9 %copy-done = bf16[2,2,320,2560]{3,2,1,0:T(8,128)(2,1)S(1)} copy-done((bf16[2,2,320,2560]{3,2,1,0:T(8,128)(2,1)S(1)}, bf16[2,2,320,2560]{3,2,1,0:T(8,128)(2,1)}, u32[]{:S(2)}) %copy-start) | copy-done | bytes 6553624
  74.0 7.0 %product.2 = (f32[2,48,640]{2,1,0:T(8,128)S(1)}, f32[2,48,640]{2,1,0:T(8,128)S(1)}, f32[2,48,640]{2,1,0:T(8,128)S(1)}, f32[2,48,640]{2,1,0:T(8,128)S(1)}) custom-call(s32[6]{0:T(128)S(1)} %stack.27.pos_ref.refs_0_, bf16[2,2,320,2560]{3,2,1,0:T(8,128)(2,1)S(1)} %copy-done, bf16[2,192,640]{2,1,0:T(8,128)(2,1)} %prep_low.3.refs_2_, ...), custom_call_target="tpu_custom_call" | custom-call | flops 2516582400 | bytes 10485760 | tf_op jit(solution)/shard_map/product/pallas_call | solution.py:270
  81.2 1.6 collective-permute-start.14
  83.0 1.6 prep_shares.1
  85.7 4.3 %collective-permute-done.14.refs_5_ = f32[2,48,640]{2,1,0:T(8,128)S(1)} collective-permute-done((f32[2,48,640]{2,1,0:T(8,128)S(1)}, f32[2,48,640]{2,1,0:T(8,128)S(1)}, u32[]{:S(2)}, u32[]{:S(2)}) %collective-permute-start.14) | collective-permute-done | bytes 245792 | tf_op jit(solution)/shard_map/ppermute | solution.py:596
  90.1 1.5 collective-permute-start.20
  91.6 2.8 %collective-permute-done.15.refs_6_ = f32[2,48,640]{2,1,0:T(8,128)S(1)} collective-permute-done((f32[2,48,640]{2,1,0:T(8,128)S(1)}, f32[2,48,640]{2,1,0:T(8,128)S(1)}, u32[]{:S(2)}, u32[]{:S(2)}) %collective-permute-start.15) | collective-permute-done | bytes 245792 | tf_op jit(solution)/shard_map/ppermute | solution.py:596
  94.4 1.9 collective-permute-start.21
  96.3 3.1 %gate_sum.1 = (f32[2,48,640]{2,1,0:T(8,128)S(1)}, f32[2,48,640]{2,1,0:T(8,128)S(1)}, f32[2,48,640]{2,1,0:T(8,128)S(1)}, f32[2,48,640]{2,1,0:T(8,128)S(1)}, f32[32,2,128]{2,1,0:T(2,128)}) custom-call(s32[6]{0:T(128)S(1)} %stack.27.pos_ref.refs_0_, s32[192,320]{1,0:T(8,128)S(1)} %bitcast.18, f32[1,128]{1,0:T(1,128)S(1)} %get-tuple-element.46.refs_2_, ...), custom_call_target="tpu_custom_call" | custom-call | flops 9830400 | bytes 1966080 | tf_op jit(solution)/shard_map/gate_sum/pallas_call | solution.py:442
  101.5 10.2 %all-to-all-start = ((f32[32,2,128]{2,1,0:T(2,128)}), f32[32,2,128]{2,1,0:T(2,128)S(1)}, u32[]{:S(2)}, u32[]{:S(2)}) async-start(f32[32,2,128]{2,1,0:T(2,128)} %get-tuple-element.51), calls=%async_computation | async-start | bytes 65536 | tf_op jit(solution)/shard_map/all_to_all | solution.py:642
  111.7 7.2 %all-to-all-done.refs_1_.refs_2_.t_ref = f32[32,2,128]{2,1,0:T(2,128)S(1)} async-done(((f32[32,2,128]{2,1,0:T(2,128)}), f32[32,2,128]{2,1,0:T(2,128)S(1)}, u32[]{:S(2)}, u32[]{:S(2)}) %all-to-all-start) | async-done | bytes 32800 | tf_op jit(solution)/shard_map/all_to_all | solution.py:642
  120.2 2.9 %copy-done.1 = bf16[2,2,320,2560]{3,2,1,0:T(8,128)(2,1)S(1)} copy-done((bf16[2,2,320,2560]{3,2,1,0:T(8,128)(2,1)S(1)}, bf16[2,2,320,2560]{3,2,1,0:T(8,128)(2,1)}, u32[]{:S(2)}) %copy-start.1) | copy-done | bytes 6553624
  124.0 3.2 %gate.2 = (f32[2,48,640]{2,1,0:T(8,128)S(1)}, f32[2,48,640]{2,1,0:T(8,128)S(1)}, f32[2,48,640]{2,1,0:T(8,128)S(1)}, f32[2,48,640]{2,1,0:T(8,128)S(1)}) custom-call(s32[6]{0:T(128)S(1)} %stack.27.pos_ref.refs_0_, s32[192,320]{1,0:T(8,128)S(1)} %bitcast.19, bf16[2,2,320,2560]{3,2,1,0:T(8,128)(2,1)S(1)} %copy-done.1, f32[2,48,640]{2,1,0:T(8,128)S(1)} %copy-done.25, ...), custom_call_target="tpu_custom_call" | custom-call | flops 9830400 | bytes 1966080 | tf_op jit(solution)/shard_map/gate/pallas_call | solution.py:442
  127.2 2.8 %gate_mix.1 = (bf16[2,48,640]{2,1,0:T(8,128)(2,1)S(1)}, bf16[2,48,640]{2,1,0:T(8,128)(2,1)S(1)}, bf16[2,48,640]{2,1,0:T(8,128)(2,1)S(1)}, bf16[2,48,640]{2,1,0:T(8,128)(2,1)S(1)}) custom-call(s32[6]{0:T(128)S(1)} %stack.27.pos_ref.refs_0_, s32[192,320]{1,0:T(8,128)S(1)} %bitcast.20, f32[32,2,128]{2,1,0:T(2,128)S(1)} %all-to-all-done.refs_1_.refs_2_.t_ref, ...), custom_call_target="tpu_custom_call" | custom-call | flops 9830400 | bytes 1966080 | tf_op jit(solution)/shard_map/gate_mix/pallas_call | solution.py:442
  132.7 1.3 collective-permute-start.35
  134.0 2.4 collective-permute-done.23.refs_3_
  136.4 1.5 collective-permute-done.24.refs_4_
  138.5 2.8 %collective-permute-start.26 = (bf16[2,192,640]{2,1,0:T(8,128)(2,1)S(1)}, bf16[2,192,640]{2,1,0:T(8,128)(2,1)S(1)}, u32[]{:S(2)}, u32[]{:S(2)}) collective-permute-start(bf16[2,192,640]{2,1,0:T(8,128)(2,1)S(1)} %join.1.refs_2_), channel_id=1, source_target_pairs={{0,2},{1,3},{2,0},{3,1},{4,6},{5,7},{6,4},{7,5},{8,10},{9,11},{10,... | collective-permute-start | bytes 1474568 | tf_op jit(solution)/shard_map/ppermute | solution.py:617
  143.9 2.1 collective-permute-done.34.refs_3_
  146.7 6.5 %collective-permute-done.26.refs_4_ = bf16[2,192,640]{2,1,0:T(8,128)(2,1)S(1)} collective-permute-done((bf16[2,192,640]{2,1,0:T(8,128)(2,1)S(1)}, bf16[2,192,640]{2,1,0:T(8,128)(2,1)S(1)}, u32[]{:S(2)}, u32[]{:S(2)}) %collective-permute-start.26) | collective-permute-done | bytes 491552 | tf_op jit(solution)/shard_map/ppermute | solution.py:617
  156.6 10.5 %collective-permute-done.36.refs_7_ = bf16[2,192,640]{2,1,0:T(8,128)(2,1)S(1)} collective-permute-done((bf16[2,192,640]{2,1,0:T(8,128)(2,1)S(1)}, bf16[2,192,640]{2,1,0:T(8,128)(2,1)S(1)}, u32[]{:S(2)}, u32[]{:S(2)}) %collective-permute-start.36) | collective-permute-done | bytes 491552 | tf_op jit(solution)/shard_map/ppermute | solution.py:617
  167.7 9.3 %collective-permute-done.38.refs_9_ = bf16[2,192,640]{2,1,0:T(8,128)(2,1)S(1)} collective-permute-done((bf16[2,192,640]{2,1,0:T(8,128)(2,1)S(1)}, bf16[2,192,640]{2,1,0:T(8,128)(2,1)S(1)}, u32[]{:S(2)}, u32[]{:S(2)}) %collective-permute-start.38) | collective-permute-done | bytes 491552 | tf_op jit(solution)/shard_map/ppermute | solution.py:617
  179.1 6.9 %product.3 = (f32[2,48,640]{2,1,0:T(8,128)S(1)}, f32[2,48,640]{2,1,0:T(8,128)S(1)}, f32[2,48,640]{2,1,0:T(8,128)S(1)}, f32[2,48,640]{2,1,0:T(8,128)S(1)}) custom-call(s32[6]{0:T(128)S(1)} %stack.27.pos_ref.refs_0_, bf16[2,2,320,2560]{3,2,1,0:T(8,128)(2,1)S(1)} %copy-done.2, bf16[2,192,640]{2,1,0:T(8,128)(2,1)S(1)} %prep_low.2.refs_2_, ...), custom_call_target="tpu_custom_call" | custom-call | flops 2516582400 | bytes 10485760 | tf_op jit(solution)/shard_map/product/pallas_call | solution.py:270
  186.0 1.8 collective-permute-start.27
  188.7 3.6 %collective-permute-done.32 = bf16[2,192,640]{2,1,0:T(8,128)(2,1)S(1)} collective-permute-done((bf16[2,192,640]{2,1,0:T(8,128)(2,1)S(1)}, bf16[2,192,640]{2,1,0:T(8,128)(2,1)S(1)}, u32[]{:S(2)}, u32[]{:S(2)}) %collective-permute-start.32) | collective-permute-done | bytes 491552 | tf_op jit(solution)/shard_map/ppermute | solution.py:617
  192.4 1.4 collective-permute-start.30
  193.7 3.2 %collective-permute-done.40.refs_4_ = f32[2,48,640]{2,1,0:T(8,128)S(1)} collective-permute-done((f32[2,48,640]{2,1,0:T(8,128)S(1)}, f32[2,48,640]{2,1,0:T(8,128)S(1)}, u32[]{:S(2)}, u32[]{:S(2)}) %collective-permute-start.40) | collective-permute-done | bytes 245792 | tf_op jit(solution)/shard_map/ppermute | solution.py:596
  196.9 4.2 %collective-permute-done.41.refs_5_ = f32[2,48,640]{2,1,0:T(8,128)S(1)} collective-permute-done((f32[2,48,640]{2,1,0:T(8,128)S(1)}, f32[2,48,640]{2,1,0:T(8,128)S(1)}, u32[]{:S(2)}, u32[]{:S(2)}) %collective-permute-start.41) | collective-permute-done | bytes 245792 | tf_op jit(solution)/shard_map/ppermute | solution.py:596
  201.9 2.4 gate.3
  204.3 4.2 %collective-permute-done.18.refs_8_.refs_7_ = f32[2,48,640]{2,1,0:T(8,128)S(1)} collective-permute-done((f32[2,48,640]{2,1,0:T(8,128)S(1)}, f32[2,48,640]{2,1,0:T(8,128)S(1)}, u32[]{:S(2)}, u32[]{:S(2)}) %collective-permute-start.18) | collective-permute-done | bytes 245792 | tf_op jit(solution)/shard_map/ppermute | solution.py:596
  210.8 2.5 %update.1 = (f32[2,2,192,320]{3,2,1,0:T(8,128)}, f32[2,2,192,320]{3,2,1,0:T(8,128)}) custom-call(s32[6]{0:T(128)S(1)} %stack.27.pos_ref.refs_0_, f32[32,2,128]{2,1,0:T(2,128)S(1)} %all-to-all-done.refs_1_.refs_2_.t_ref, f32[2,2,192,320]{3,2,1,0:T(8,128)S(1)} %bitcast.23, f32[2,2,192,320]{3,2,1,0:T(8,128)S(1)} %bitcast.25, f32[2,2,192,320]{3,2,1,0:T(8,128)S(1)} %bitcast.16, ...), custom_call_target="tpu_custom_call" | custom-call | flops 983040 | bytes 5898240 | tf_op jit(solution)/shard_map/update/pallas_call | solution.py:503
  213.4 7.9 %collective-permute-done.33.refs_9_ = bf16[2,192,640]{2,1,0:T(8,128)(2,1)S(1)} collective-permute-done((bf16[2,192,640]{2,1,0:T(8,128)(2,1)S(1)}, bf16[2,192,640]{2,1,0:T(8,128)(2,1)S(1)}, u32[]{:S(2)}, u32[]{:S(2)}) %collective-permute-start.33) | collective-permute-done | bytes 491552 | tf_op jit(solution)/shard_map/ppermute | solution.py:617
  221.3 5.7 %product_back.1 = (f32[2,2,192,320]{3,2,1,0:T(8,128)S(1)}, f32[1,128]{1,0:T(1,128)S(1)}) custom-call(s32[6]{0:T(128)S(1)} %stack.27.pos_ref.refs_0_, bf16[2,2,320,2560]{3,2,1,0:T(8,128)(2,1)S(1)} %copy-done.2, bf16[2,192,640]{2,1,0:T(8,128)(2,1)S(1)} %join.1.refs_2_, bf16[2,192,640]{2,1,0:T(8,128)(2,1)S(1)} %collective-permute-done.25.refs_3_, ...), custom_call_target="tpu_custom_call" | custom-call | flops 2516582400 | bytes 10485760 | tf_op jit(solution)/shard_map/product_back/pallas_call | solution.py:270
  227.1 2.4 %green.1 = (f32[2,2,192,320]{3,2,1,0:T(8,128)}, f32[32,8,128]{2,1,0:T(8,128)S(1)}) custom-call(s32[6]{0:T(128)S(1)} %stack.27.pos_ref.refs_0_, f32[32,2,128]{2,1,0:T(2,128)S(1)} %all-to-all-done.refs_1_.refs_2_.t_ref, f32[2,2,192,320]{3,2,1,0:T(8,128)S(1)} %copy-done.9, f32[1,128]{1,0:T(1,128)S(1)} %get-tuple-element.71.refs_3_, ...), custom_call_target="tpu_custom_call" | custom-call | flops 2949120 | bytes 5898240 | tf_op jit(solution)/shard_map/green/pallas_call | solution.py:546
  229.5 10.8 %all_to_all.10.g_ref = f32[32,8,128]{2,1,0:T(8,128)S(1)} all-to-all(f32[32,8,128]{2,1,0:T(8,128)S(1)} %get-tuple-element.82), channel_id=1, replica_groups=mesh['freq'=4,'rcv'=8] {'freq','rcv'}, dimensions={0} | all-to-all | bytes 262144 | tf_op jit(solution)/shard_map/all_to_all | solution.py:642
  240.3 1.9 turn.1
  (120 shorter events, 33.7 us)
Async XLA Ops:
  3.4 14.6 %collective-permute-start.5 = (bf16[2,192,640]{2,1,0:T(8,128)(2,1)}, bf16[2,192,640]{2,1,0:T(8,128)(2,1)}, u32[]{:S(2)}, u32[]{:S(2)}) collective-permute-start(bf16[2,192,640]{2,1,0:T(8,128)(2,1)} %prep_low.3.refs_2_), channel_id=1, source_target_pairs={{0,2},{1,3},{2,0},{3,1},{4,6},{5,7},{6,4},{7,5},{8,10},{9,11},{10,... | collective-permute-start | bytes 1474568 | tf_op jit(solution)/shard_map/ppermute | solution.py:617
  6.5 12.2 %collective-permute-start.7 = (bf16[2,192,640]{2,1,0:T(8,128)(2,1)}, bf16[2,192,640]{2,1,0:T(8,128)(2,1)S(1)}, u32[]{:S(2)}, u32[]{:S(2)}) collective-permute-start(bf16[2,192,640]{2,1,0:T(8,128)(2,1)} %prep_low.3.refs_2_), channel_id=1, source_target_pairs={{2,4},{3,5},{4,2},{5,3},{10,12},{11,13},{12,10},{13,11},{18,20},{1... | collective-permute-start | bytes 1474568 | tf_op jit(solution)/shard_map/ppermute | solution.py:617
  18.0 2.0 collective-permute-start.10
  18.7 20.5 %collective-permute-start.8 = (bf16[2,192,640]{2,1,0:T(8,128)(2,1)S(1)}, bf16[2,192,640]{2,1,0:T(8,128)(2,1)}, u32[]{:S(2)}, u32[]{:S(2)}) collective-permute-start(bf16[2,192,640]{2,1,0:T(8,128)(2,1)S(1)} %collective-permute-done.7), channel_id=1, source_target_pairs={{2,0},{3,1},{4,6},{5,7},{10,8},{11,9},{12,14},{13,15},{18,16},{19,... | collective-permute-start | bytes 1474568 | tf_op jit(solution)/shard_map/ppermute | solution.py:617
  20.0 27.3 %collective-permute-start.11 = (bf16[2,192,640]{2,1,0:T(8,128)(2,1)S(1)}, bf16[2,192,640]{2,1,0:T(8,128)(2,1)S(1)}, u32[]{:S(2)}, u32[]{:S(2)}) collective-permute-start(bf16[2,192,640]{2,1,0:T(8,128)(2,1)S(1)} %collective-permute-done.10), channel_id=1, source_target_pairs={{2,0},{3,1},{4,6},{5,7},{10,8},{11,9},{12,14},{13,15},{18,16},{19,... | collective-permute-start | bytes 1474568 | tf_op jit(solution)/shard_map/ppermute | solution.py:617
  21.3 29.6 %collective-permute-start.4 = (bf16[2,192,640]{2,1,0:T(8,128)(2,1)}, bf16[2,192,640]{2,1,0:T(8,128)(2,1)}, u32[]{:S(2)}, u32[]{:S(2)}) collective-permute-start(bf16[2,192,640]{2,1,0:T(8,128)(2,1)} %prep_low.3.refs_2_), channel_id=1, source_target_pairs={{0,1},{1,0},{2,3},{3,2},{4,5},{5,4},{6,7},{7,6},{8,9},{9,8},{10,11... | collective-permute-start | bytes 1474568 | tf_op jit(solution)/shard_map/ppermute | solution.py:617
  23.9 31.9 %collective-permute-start = (bf16[2,192,640]{2,1,0:T(8,128)(2,1)S(1)}, bf16[2,192,640]{2,1,0:T(8,128)(2,1)}, u32[]{:S(2)}, u32[]{:S(2)}) collective-permute-start(bf16[2,192,640]{2,1,0:T(8,128)(2,1)S(1)} %prep_low.2.refs_2_), channel_id=1, source_target_pairs={{0,2},{1,3},{2,0},{3,1},{4,6},{5,7},{6,4},{7,5},{8,10},{9,11},{10,... | collective-permute-start | bytes 1474568 | tf_op jit(solution)/shard_map/ppermute | solution.py:617
  37.7 19.5 %collective-permute-start.2 = (bf16[2,192,640]{2,1,0:T(8,128)(2,1)S(1)}, bf16[2,192,640]{2,1,0:T(8,128)(2,1)}, u32[]{:S(2)}, u32[]{:S(2)}) collective-permute-start(bf16[2,192,640]{2,1,0:T(8,128)(2,1)S(1)} %prep_low.2.refs_2_), channel_id=1, source_target_pairs={{2,4},{3,5},{4,2},{5,3},{10,12},{11,13},{12,10},{13,11},{18,20},{1... | collective-permute-start | bytes 1474568 | tf_op jit(solution)/shard_map/ppermute | solution.py:617
  39.2 19.3 %collective-permute-start.6 = (bf16[2,192,640]{2,1,0:T(8,128)(2,1)}, bf16[2,192,640]{2,1,0:T(8,128)(2,1)S(1)}, u32[]{:S(2)}, u32[]{:S(2)}) collective-permute-start(bf16[2,192,640]{2,1,0:T(8,128)(2,1)} %collective-permute-done.5.refs_4_), channel_id=1, source_target_pairs={{0,1},{1,0},{2,3},{3,2},{4,5},{5,4},{6,7},{7,6},{8,9},{9,8},{10,11... | collective-permute-start | bytes 1474568 | tf_op jit(solution)/shard_map/ppermute | solution.py:617
  39.7 43.3 %copy-start.8 = (f32[2,320,2,192]{1,3,2,0:T(8,128)S(1)}, f32[2,320,2,192]{1,3,2,0:T(8,128)}, u32[]{:S(2)}) copy-start(f32[2,320,2,192]{1,3,2,0:T(8,128)} %param.11) | copy-start | bytes 2949124
  48.1 15.9 %collective-permute-start.9 = (bf16[2,192,640]{2,1,0:T(8,128)(2,1)S(1)}, bf16[2,192,640]{2,1,0:T(8,128)(2,1)S(1)}, u32[]{:S(2)}, u32[]{:S(2)}) collective-permute-start(bf16[2,192,640]{2,1,0:T(8,128)(2,1)S(1)} %broadcast_select_fusion.5.refs_6_), channel_id=1, source_target_pairs={{0,1},{1,0},{2,3},{3,2},{4,5},{5,4},{6,7},{7,6},{8,9},{9,8},{10,11... | collective-permute-start | bytes 1474568 | tf_op jit(solution)/shard_map/ppermute | solution.py:617
  50.9 20.2 %collective-permute-start.12 = (bf16[2,192,640]{2,1,0:T(8,128)(2,1)S(1)}, bf16[2,192,640]{2,1,0:T(8,128)(2,1)S(1)}, u32[]{:S(2)}, u32[]{:S(2)}) collective-permute-start(bf16[2,192,640]{2,1,0:T(8,128)(2,1)S(1)} %broadcast_select_fusion.4.refs_8_), channel_id=1, source_target_pairs={{0,1},{1,0},{2,3},{3,2},{4,5},{5,4},{6,7},{7,6},{8,9},{9,8},{10,11... | collective-permute-start | bytes 1474568 | tf_op jit(solution)/shard_map/ppermute | solution.py:617
  55.8 55.9 %collective-permute-start.1 = (bf16[2,192,640]{2,1,0:T(8,128)(2,1)}, bf16[2,192,640]{2,1,0:T(8,128)(2,1)}, u32[]{:S(2)}, u32[]{:S(2)}) collective-permute-start(bf16[2,192,640]{2,1,0:T(8,128)(2,1)} %collective-permute-done.refs_4_), channel_id=1, source_target_pairs={{2,4},{3,5},{4,2},{5,3},{10,12},{11,13},{12,10},{13,11},{18,20},{1... | collective-permute-start | bytes 1474568 | tf_op jit(solution)/shard_map/ppermute | solution.py:617
  57.2 54.4 %collective-permute-start.3 = (bf16[2,192,640]{2,1,0:T(8,128)(2,1)}, bf16[2,192,640]{2,1,0:T(8,128)(2,1)}, u32[]{:S(2)}, u32[]{:S(2)}) collective-permute-start(bf16[2,192,640]{2,1,0:T(8,128)(2,1)} %collective-permute-done.2), channel_id=1, source_target_pairs={{2,0},{3,1},{4,6},{5,7},{10,8},{11,9},{12,14},{13,15},{18,16},{19,... | collective-permute-start | bytes 1474568 | tf_op jit(solution)/shard_map/ppermute | solution.py:617
  81.1 4.3 %collective-permute-start.13 = (f32[2,48,640]{2,1,0:T(8,128)S(1)}, f32[2,48,640]{2,1,0:T(8,128)S(1)}, u32[]{:S(2)}, u32[]{:S(2)}) collective-permute-start(f32[2,48,640]{2,1,0:T(8,128)S(1)} %get-tuple-element.48.refs_13_), channel_id=1, source_target_pairs={{0,8},{8,0},{16,24},{24,16},{1,9},{9,1},{17,25},{25,17},{2,10},{10... | collective-permute-start | bytes 737288 | tf_op jit(solution)/shard_map/ppermute | solution.py:596
  81.2 8.9 %collective-permute-start.14 = (f32[2,48,640]{2,1,0:T(8,128)S(1)}, f32[2,48,640]{2,1,0:T(8,128)S(1)}, u32[]{:S(2)}, u32[]{:S(2)}) collective-permute-start(f32[2,48,640]{2,1,0:T(8,128)S(1)} %get-tuple-element.49.refs_14_), channel_id=1, source_target_pairs={{0,16},{8,24},{16,0},{24,8},{1,17},{9,25},{17,1},{25,9},{2,18},{10... | collective-permute-start | bytes 737288 | tf_op jit(solution)/shard_map/ppermute | solution.py:596
  82.7 11.6 %collective-permute-start.15 = (f32[2,48,640]{2,1,0:T(8,128)S(1)}, f32[2,48,640]{2,1,0:T(8,128)S(1)}, u32[]{:S(2)}, u32[]{:S(2)}) collective-permute-start(f32[2,48,640]{2,1,0:T(8,128)S(1)} %get-tuple-element.50.refs_15_), channel_id=1, source_target_pairs={{0,24},{8,16},{16,8},{24,0},{1,25},{9,17},{17,9},{25,1},{2,26},{10... | collective-permute-start | bytes 737288 | tf_op jit(solution)/shard_map/ppermute | solution.py:596
  85.4 34.7 %collective-permute-start.19 = (f32[2,48,640]{2,1,0:T(8,128)}, f32[2,48,640]{2,1,0:T(8,128)}, u32[]{:S(2)}, u32[]{:S(2)}) collective-permute-start(f32[2,48,640]{2,1,0:T(8,128)} %get-tuple-element.60), channel_id=1, source_target_pairs={{0,8},{8,0},{16,24},{24,16},{1,9},{9,1},{17,25},{25,17},{2,10},{10... | collective-permute-start | bytes 737288 | tf_op jit(solution)/shard_map/ppermute | solution.py:596
  90.1 30.1 %collective-permute-start.20 = (f32[2,48,640]{2,1,0:T(8,128)}, f32[2,48,640]{2,1,0:T(8,128)}, u32[]{:S(2)}, u32[]{:S(2)}) collective-permute-start(f32[2,48,640]{2,1,0:T(8,128)} %get-tuple-element.61), channel_id=1, source_target_pairs={{0,16},{8,24},{16,0},{24,8},{1,17},{9,25},{17,1},{25,9},{2,18},{10... | collective-permute-start | bytes 737288 | tf_op jit(solution)/shard_map/ppermute | solution.py:596
  94.4 25.8 %collective-permute-start.21 = (f32[2,48,640]{2,1,0:T(8,128)}, f32[2,48,640]{2,1,0:T(8,128)}, u32[]{:S(2)}, u32[]{:S(2)}) collective-permute-start(f32[2,48,640]{2,1,0:T(8,128)} %get-tuple-element.62), channel_id=1, source_target_pairs={{0,24},{8,16},{16,8},{24,0},{1,25},{9,17},{17,9},{25,1},{2,26},{10... | collective-permute-start | bytes 737288 | tf_op jit(solution)/shard_map/ppermute | solution.py:596
  101.5 17.4 %all-to-all-start = ((f32[32,2,128]{2,1,0:T(2,128)}), f32[32,2,128]{2,1,0:T(2,128)S(1)}, u32[]{:S(2)}, u32[]{:S(2)}) async-start(f32[32,2,128]{2,1,0:T(2,128)} %get-tuple-element.51), calls=%async_computation | async-start | bytes 65536 | tf_op jit(solution)/shard_map/all_to_all | solution.py:642
  118.8 24.3 %collective-permute-start.37 = (bf16[2,192,640]{2,1,0:T(8,128)(2,1)}, bf16[2,192,640]{2,1,0:T(8,128)(2,1)S(1)}, u32[]{:S(2)}, u32[]{:S(2)}) collective-permute-start(bf16[2,192,640]{2,1,0:T(8,128)(2,1)} %collective-permute-done.1), channel_id=1, source_target_pairs={{2,0},{3,1},{4,6},{5,7},{10,8},{11,9},{12,14},{13,15},{18,16},{19,... | collective-permute-start | bytes 1474568 | tf_op jit(solution)/shard_map/ppermute | solution.py:617
  124.0 55.1 %copy-start.2 = (bf16[2,2,320,2560]{3,2,1,0:T(8,128)(2,1)S(1)}, bf16[2,2,320,2560]{3,2,1,0:T(8,128)(2,1)}, u32[]{:S(2)}) copy-start(bf16[2,2,320,2560]{3,2,1,0:T(8,128)(2,1)} %refs_1_.5) | copy-start | bytes 19660804
  130.0 2.6 %collective-permute-start.22 = (bf16[2,48,640]{2,1,0:T(8,128)(2,1)S(1)}, bf16[2,48,640]{2,1,0:T(8,128)(2,1)S(1)}, u32[]{:S(2)}, u32[]{:S(2)}) collective-permute-start(bf16[2,48,640]{2,1,0:T(8,128)(2,1)S(1)} %get-tuple-element.68), channel_id=1, source_target_pairs={{0,8},{8,0},{16,24},{24,16},{1,9},{9,1},{17,25},{25,17},{2,10},{10... | collective-permute-start | bytes 368648 | tf_op jit(solution)/shard_map/ppermute | solution.py:596
  130.2 6.2 %collective-permute-start.23 = (bf16[2,48,640]{2,1,0:T(8,128)(2,1)S(1)}, bf16[2,48,640]{2,1,0:T(8,128)(2,1)S(1)}, u32[]{:S(2)}, u32[]{:S(2)}) collective-permute-start(bf16[2,48,640]{2,1,0:T(8,128)(2,1)S(1)} %get-tuple-element.69), channel_id=1, source_target_pairs={{0,16},{8,24},{16,0},{24,8},{1,17},{9,25},{17,1},{25,9},{2,18},{10... | collective-permute-start | bytes 368648 | tf_op jit(solution)/shard_map/ppermute | solution.py:596
  130.8 7.1 %collective-permute-start.24 = (bf16[2,48,640]{2,1,0:T(8,128)(2,1)S(1)}, bf16[2,48,640]{2,1,0:T(8,128)(2,1)S(1)}, u32[]{:S(2)}, u32[]{:S(2)}) collective-permute-start(bf16[2,48,640]{2,1,0:T(8,128)(2,1)S(1)} %get-tuple-element.70), channel_id=1, source_target_pairs={{0,24},{8,16},{16,8},{24,0},{1,25},{9,17},{17,9},{25,1},{2,26},{10... | collective-permute-start | bytes 368648 | tf_op jit(solution)/shard_map/ppermute | solution.py:596
  131.9 14.1 %collective-permute-start.34 = (bf16[2,192,640]{2,1,0:T(8,128)(2,1)S(1)}, bf16[2,192,640]{2,1,0:T(8,128)(2,1)S(1)}, u32[]{:S(2)}, u32[]{:S(2)}) collective-permute-start(bf16[2,192,640]{2,1,0:T(8,128)(2,1)S(1)} %prep_low.2.refs_2_), channel_id=1, source_target_pairs={{0,1},{1,0},{2,3},{3,2},{4,5},{5,4},{6,7},{7,6},{8,9},{9,8},{10,11... | collective-permute-start | bytes 1474568 | tf_op jit(solution)/shard_map/ppermute | solution.py:617
  132.7 23.9 %collective-permute-start.35 = (bf16[2,192,640]{2,1,0:T(8,128)(2,1)}, bf16[2,192,640]{2,1,0:T(8,128)(2,1)S(1)}, u32[]{:S(2)}, u32[]{:S(2)}) collective-permute-start(bf16[2,192,640]{2,1,0:T(8,128)(2,1)} %collective-permute-done.refs_4_), channel_id=1, source_target_pairs={{0,1},{1,0},{2,3},{3,2},{4,5},{5,4},{6,7},{7,6},{8,9},{9,8},{10,11... | collective-permute-start | bytes 1474568 | tf_op jit(solution)/shard_map/ppermute | solution.py:617
  138.5 14.8 %collective-permute-start.26 = (bf16[2,192,640]{2,1,0:T(8,128)(2,1)S(1)}, bf16[2,192,640]{2,1,0:T(8,128)(2,1)S(1)}, u32[]{:S(2)}, u32[]{:S(2)}) collective-permute-start(bf16[2,192,640]{2,1,0:T(8,128)(2,1)S(1)} %join.1.refs_2_), channel_id=1, source_target_pairs={{0,2},{1,3},{2,0},{3,1},{4,6},{5,7},{6,4},{7,5},{8,10},{9,11},{10,... | collective-permute-start | bytes 1474568 | tf_op jit(solution)/shard_map/ppermute | solution.py:617
  142.3 24.8 %collective-permute-start.36 = (bf16[2,192,640]{2,1,0:T(8,128)(2,1)S(1)}, bf16[2,192,640]{2,1,0:T(8,128)(2,1)S(1)}, u32[]{:S(2)}, u32[]{:S(2)}) collective-permute-start(bf16[2,192,640]{2,1,0:T(8,128)(2,1)S(1)} %broadcast_select_fusion.1.refs_6_), channel_id=1, source_target_pairs={{0,1},{1,0},{2,3},{3,2},{4,5},{5,4},{6,7},{7,6},{8,9},{9,8},{10,11... | collective-permute-start | bytes 1474568 | tf_op jit(solution)/shard_map/ppermute | solution.py:617
  143.1 10.9 %collective-permute-start.28 = (bf16[2,192,640]{2,1,0:T(8,128)(2,1)S(1)}, bf16[2,192,640]{2,1,0:T(8,128)(2,1)S(1)}, u32[]{:S(2)}, u32[]{:S(2)}) collective-permute-start(bf16[2,192,640]{2,1,0:T(8,128)(2,1)S(1)} %join.1.refs_2_), channel_id=1, source_target_pairs={{2,4},{3,5},{4,2},{5,3},{10,12},{11,13},{12,10},{13,11},{18,20},{1... | collective-permute-start | bytes 1474568 | tf_op jit(solution)/shard_map/ppermute | solution.py:617
  146.0 31.0 %collective-permute-start.38 = (bf16[2,192,640]{2,1,0:T(8,128)(2,1)S(1)}, bf16[2,192,640]{2,1,0:T(8,128)(2,1)S(1)}, u32[]{:S(2)}, u32[]{:S(2)}) collective-permute-start(bf16[2,192,640]{2,1,0:T(8,128)(2,1)S(1)} %broadcast_select_fusion.refs_8_), channel_id=1, source_target_pairs={{0,1},{1,0},{2,3},{3,2},{4,5},{5,4},{6,7},{7,6},{8,9},{9,8},{10,11... | collective-permute-start | bytes 1474568 | tf_op jit(solution)/shard_map/ppermute | solution.py:617
  153.3 24.5 %collective-permute-start.31 = (bf16[2,192,640]{2,1,0:T(8,128)(2,1)S(1)}, bf16[2,192,640]{2,1,0:T(8,128)(2,1)S(1)}, u32[]{:S(2)}, u32[]{:S(2)}) collective-permute-start(bf16[2,192,640]{2,1,0:T(8,128)(2,1)S(1)} %collective-permute-done.26.refs_4_), channel_id=1, source_target_pairs={{2,4},{3,5},{4,2},{5,3},{10,12},{11,13},{12,10},{13,11},{18,20},{1... | collective-permute-start | bytes 1474568 | tf_op jit(solution)/shard_map/ppermute | solution.py:617
  154.0 32.0 %collective-permute-start.29 = (bf16[2,192,640]{2,1,0:T(8,128)(2,1)S(1)}, bf16[2,192,640]{2,1,0:T(8,128)(2,1)S(1)}, u32[]{:S(2)}, u32[]{:S(2)}) collective-permute-start(bf16[2,192,640]{2,1,0:T(8,128)(2,1)S(1)} %collective-permute-done.28), channel_id=1, source_target_pairs={{2,0},{3,1},{4,6},{5,7},{10,8},{11,9},{12,14},{13,15},{18,16},{19,... | collective-permute-start | bytes 1474568 | tf_op jit(solution)/shard_map/ppermute | solution.py:617
  156.6 31.4 %collective-permute-start.16 = (f32[2,48,640]{2,1,0:T(8,128)S(1)}, f32[2,48,640]{2,1,0:T(8,128)S(1)}, u32[]{:S(2)}, u32[]{:S(2)}) collective-permute-start(f32[2,48,640]{2,1,0:T(8,128)S(1)} %copy-done.23), channel_id=1, source_target_pairs={{0,8},{8,0},{16,24},{24,16},{1,9},{9,1},{17,25},{25,17},{2,10},{10... | collective-permute-start | bytes 737288 | tf_op jit(solution)/shard_map/ppermute | solution.py:596
  167.1 20.9 %collective-permute-start.17 = (f32[2,48,640]{2,1,0:T(8,128)S(1)}, f32[2,48,640]{2,1,0:T(8,128)S(1)}, u32[]{:S(2)}, u32[]{:S(2)}) collective-permute-start(f32[2,48,640]{2,1,0:T(8,128)S(1)} %copy-done.21), channel_id=1, source_target_pairs={{0,16},{8,24},{16,0},{24,8},{1,17},{9,25},{17,1},{25,9},{2,18},{10... | collective-permute-start | bytes 737288 | tf_op jit(solution)/shard_map/ppermute | solution.py:596
  177.1 32.4 %collective-permute-start.25 = (bf16[2,192,640]{2,1,0:T(8,128)(2,1)S(1)}, bf16[2,192,640]{2,1,0:T(8,128)(2,1)S(1)}, u32[]{:S(2)}, u32[]{:S(2)}) collective-permute-start(bf16[2,192,640]{2,1,0:T(8,128)(2,1)S(1)} %join.1.refs_2_), channel_id=1, source_target_pairs={{0,1},{1,0},{2,3},{3,2},{4,5},{5,4},{6,7},{7,6},{8,9},{9,8},{10,11... | collective-permute-start | bytes 1474568 | tf_op jit(solution)/shard_map/ppermute | solution.py:617
  177.8 14.5 %collective-permute-start.32 = (bf16[2,192,640]{2,1,0:T(8,128)(2,1)S(1)}, bf16[2,192,640]{2,1,0:T(8,128)(2,1)S(1)}, u32[]{:S(2)}, u32[]{:S(2)}) collective-permute-start(bf16[2,192,640]{2,1,0:T(8,128)(2,1)S(1)} %collective-permute-done.31), channel_id=1, source_target_pairs={{2,0},{3,1},{4,6},{5,7},{10,8},{11,9},{12,14},{13,15},{18,16},{19,... | collective-permute-start | bytes 1474568 | tf_op jit(solution)/shard_map/ppermute | solution.py:617
  186.0 24.0 %collective-permute-start.27 = (bf16[2,192,640]{2,1,0:T(8,128)(2,1)S(1)}, bf16[2,192,640]{2,1,0:T(8,128)(2,1)S(1)}, u32[]{:S(2)}, u32[]{:S(2)}) collective-permute-start(bf16[2,192,640]{2,1,0:T(8,128)(2,1)S(1)} %collective-permute-done.26.refs_4_), channel_id=1, source_target_pairs={{0,1},{1,0},{2,3},{3,2},{4,5},{5,4},{6,7},{7,6},{8,9},{9,8},{10,11... | collective-permute-start | bytes 1474568 | tf_op jit(solution)/shard_map/ppermute | solution.py:617
  187.9 4.4 %collective-permute-start.39 = (f32[2,48,640]{2,1,0:T(8,128)S(1)}, f32[2,48,640]{2,1,0:T(8,128)S(1)}, u32[]{:S(2)}, u32[]{:S(2)}) collective-permute-start(f32[2,48,640]{2,1,0:T(8,128)S(1)} %get-tuple-element.75.refs_17_), channel_id=1, source_target_pairs={{0,8},{8,0},{16,24},{24,16},{1,9},{9,1},{17,25},{25,17},{2,10},{10... | collective-permute-start | bytes 737288 | tf_op jit(solution)/shard_map/ppermute | solution.py:596
  188.0 8.9 %collective-permute-start.40 = (f32[2,48,640]{2,1,0:T(8,128)S(1)}, f32[2,48,640]{2,1,0:T(8,128)S(1)}, u32[]{:S(2)}, u32[]{:S(2)}) collective-permute-start(f32[2,48,640]{2,1,0:T(8,128)S(1)} %get-tuple-element.76.refs_18_), channel_id=1, source_target_pairs={{0,16},{8,24},{16,0},{24,8},{1,17},{9,25},{17,1},{25,9},{2,18},{10... | collective-permute-start | bytes 737288 | tf_op jit(solution)/shard_map/ppermute | solution.py:596
  192.3 8.8 %collective-permute-start.41 = (f32[2,48,640]{2,1,0:T(8,128)S(1)}, f32[2,48,640]{2,1,0:T(8,128)S(1)}, u32[]{:S(2)}, u32[]{:S(2)}) collective-permute-start(f32[2,48,640]{2,1,0:T(8,128)S(1)} %get-tuple-element.77.refs_19_), channel_id=1, source_target_pairs={{0,24},{8,16},{16,8},{24,0},{1,25},{9,17},{17,9},{25,1},{2,26},{10... | collective-permute-start | bytes 737288 | tf_op jit(solution)/shard_map/ppermute | solution.py:596
  192.4 21.0 %collective-permute-start.30 = (bf16[2,192,640]{2,1,0:T(8,128)(2,1)S(1)}, bf16[2,192,640]{2,1,0:T(8,128)(2,1)S(1)}, u32[]{:S(2)}, u32[]{:S(2)}) collective-permute-start(bf16[2,192,640]{2,1,0:T(8,128)(2,1)S(1)} %broadcast_select_fusion.3.refs_6_), channel_id=1, source_target_pairs={{0,1},{1,0},{2,3},{3,2},{4,5},{5,4},{6,7},{7,6},{8,9},{9,8},{10,11... | collective-permute-start | bytes 1474568 | tf_op jit(solution)/shard_map/ppermute | solution.py:617
  196.9 24.4 %collective-permute-start.33 = (bf16[2,192,640]{2,1,0:T(8,128)(2,1)S(1)}, bf16[2,192,640]{2,1,0:T(8,128)(2,1)S(1)}, u32[]{:S(2)}, u32[]{:S(2)}) collective-permute-start(bf16[2,192,640]{2,1,0:T(8,128)(2,1)S(1)} %broadcast_select_fusion.2.refs_8_), channel_id=1, source_target_pairs={{0,1},{1,0},{2,3},{3,2},{4,5},{5,4},{6,7},{7,6},{8,9},{9,8},{10,11... | collective-permute-start | bytes 1474568 | tf_op jit(solution)/shard_map/ppermute | solution.py:617
  201.1 7.4 %collective-permute-start.18 = (f32[2,48,640]{2,1,0:T(8,128)S(1)}, f32[2,48,640]{2,1,0:T(8,128)S(1)}, u32[]{:S(2)}, u32[]{:S(2)}) collective-permute-start(f32[2,48,640]{2,1,0:T(8,128)S(1)} %copy-done.19), channel_id=1, source_target_pairs={{0,24},{8,16},{16,8},{24,0},{1,25},{9,17},{17,9},{25,1},{2,26},{10... | collective-permute-start | bytes 737288 | tf_op jit(solution)/shard_map/ppermute | solution.py:596
  208.5 18.5 %collective-permute-start.42 = (f32[2,48,640]{2,1,0:T(8,128)S(1)}, f32[2,48,640]{2,1,0:T(8,128)S(1)}, u32[]{:S(2)}, u32[]{:S(2)}) collective-permute-start(f32[2,48,640]{2,1,0:T(8,128)S(1)} %get-tuple-element.79), channel_id=1, source_target_pairs={{0,8},{8,0},{16,24},{24,16},{1,9},{9,1},{17,25},{25,17},{2,10},{10... | collective-permute-start | bytes 737288 | tf_op jit(solution)/shard_map/ppermute | solution.py:596
  209.5 17.5 %collective-permute-start.43 = (f32[2,48,640]{2,1,0:T(8,128)S(1)}, f32[2,48,640]{2,1,0:T(8,128)S(1)}, u32[]{:S(2)}, u32[]{:S(2)}) collective-permute-start(f32[2,48,640]{2,1,0:T(8,128)S(1)} %get-tuple-element.80), channel_id=1, source_target_pairs={{0,16},{8,24},{16,0},{24,8},{1,17},{9,25},{17,1},{25,9},{2,18},{10... | collective-permute-start | bytes 737288 | tf_op jit(solution)/shard_map/ppermute | solution.py:596
  210.1 17.0 %collective-permute-start.44 = (f32[2,48,640]{2,1,0:T(8,128)S(1)}, f32[2,48,640]{2,1,0:T(8,128)S(1)}, u32[]{:S(2)}, u32[]{:S(2)}) collective-permute-start(f32[2,48,640]{2,1,0:T(8,128)S(1)} %get-tuple-element.81), channel_id=1, source_target_pairs={{0,24},{8,16},{16,8},{24,0},{1,25},{9,17},{17,9},{25,1},{2,26},{10... | collective-permute-start | bytes 737288 | tf_op jit(solution)/shard_map/ppermute | solution.py:596
  (25 other events, 201.7 us)
